TPU v7x, 32 devices: a whole 2x2x4 slice. The times are simulated.
32 devices in a mesh: section: 2 (over core), dp: 4 (over z), mp: 4 (over y, x).
Axes of the slice: x: 2, y: 2, z: 4, core: 2. Of those that a mesh axis runs over, the one named last changes fastest.
Arguments:
- states: bfloat16 [2, 512, 4096], P('section', 'dp'), may hold values from -6 to 6
- gains: float32 [2, 4096], P('section'), may hold values from 0.25 to 1.75
- proj_a: bfloat16 [2, 4096, 4096], P('section', None, 'mp'), may hold values from -0.03125 to 0.03125
- proj_b: bfloat16 [2, 4096, 4096], P('section', None, 'mp'), may hold values from -0.09375 to 0.09375
- cotangent: bfloat16 [512, 4096], P('dp'), may hold values from -12 to 12
- src_len: int32 [4, 16], replicated, may hold values from 1 to 16, 128 in all within a row
- tgt_len: int32 [4, 16], replicated, may hold values from 1 to 16, 128 in all within a row
- dest: int32 [4, 16], replicated, may hold values from 0 to 63, as said below
Outputs:
- grad_states: bfloat16 [2, 512, 4096], P('section', 'dp')
- grad_a: float32 [2, 4096, 4096], P('section', 'dp', 'mp')
- grad_b: float32 [2, 4096, 4096], P('section', 'dp', 'mp')
Inputs may be any that keep to these rules, and one draw needn't show every extreme that they name: `src_len`: each row sums to 128. `tgt_len`: each row sums to 128. `dest`: every value from 0 to 63 appears once; each row holds exactly 4 values in each range d * 16 to (d + 1) * 16 - 1.
All inputs are finite; a program needn't handle non-finite values.
Results may differ from a plain program's by a relative error of at most 0.014.
Values may be sent and summed in bfloat16 or wider, within the bound.
A program may use at most 128 MiB of HBM per device.

v0:
```python
import functools

import jax
import jax.numpy as jnp
from jax import lax
from jax.experimental import pallas as pl
from jax.experimental.pallas import tpu as pltpu
from jax.sharding import PartitionSpec as P

HEAD_DIM = 64
LANES = 128
EPS = 1e-06
MESH = pl.DeviceIdType.MESH


def rms_forward(states_row, gain):
    xf = states_row.astype(jnp.float32)
    scale = lax.rsqrt(jnp.mean(xf * xf, axis=-1, keepdims=True) + EPS)
    return (xf, scale, (xf * scale * gain).astype(jnp.bfloat16))


def left_product(left, right):
    return lax.dot_general(
        left, right, (((0,), (0,)), ((), ())), preferred_element_type=jnp.float32
    )


def right_product(rows, weight):
    return lax.dot_general(
        rows, weight, (((1,), (1,)), ((), ())), preferred_element_type=jnp.float32
    )


def sequence_of(lengths, names, tokens):
    slot = jnp.arange(lengths.shape[1], dtype=jnp.int32)
    before = slot[:, None] < slot[None, :]
    starts = jnp.sum(jnp.where(before[None], lengths[:, :, None], 0), axis=1)
    place = jnp.arange(tokens, dtype=jnp.int32)[None, :, None]
    offset = place - starts[:, None, :]
    inside = (offset >= 0) & (offset < lengths[:, None, :])
    return jnp.sum(jnp.where(inside, names[:, None, :], 0), axis=-1).reshape(-1)


def attend_piece(encoder, p, group, id_col, id_row, own, other, out_a, out_b, acc_a, acc_b):
    n, tokens, width = own.shape[1:]
    half = width // 2
    rows = n * tokens
    blocks = n // group
    lane = lax.broadcasted_iota(jnp.int32, (1, LANES), 1) // HEAD_DIM
    zero = jnp.zeros((), jnp.bfloat16)
    f32 = jnp.float32

    def cut(ref, which, c, at):
        lo = pl.multiple_of(which * half + c * LANES, LANES)
        return ref[p, at, :, pl.ds(lo, LANES)].reshape(-1, LANES)

    every = pl.ds(0, n)

    @pl.loop(0, half // LANES)
    def _(c):
        out_cols = pl.ds(pl.multiple_of(p * half + c * LANES, LANES), LANES)

        @pl.when(encoder)
        def _():
            keys, values = cut(own, 0, c, every), cut(own, 1, c, every)
            if blocks > 1:
                acc_a[...] = jnp.zeros_like(acc_a)
                acc_b[...] = jnp.zeros_like(acc_b)

            def block(b):
                at = pl.ds(b * group, group)
                query, dout = cut(other, 0, c, at), cut(other, 1, c, at)
                mask = id_col[...].reshape(rows, 1) == id_row[b]
                dk, dv = None, None
                for h in range(LANES // HEAD_DIM):
                    qh = jnp.where(lane == h, query, zero)
                    dh = jnp.where(lane == h, dout, zero)
                    expo = jnp.exp(jnp.where(mask, right_product(keys, qh), -jnp.inf))
                    weight = expo * (1.0 / jnp.sum(expo, axis=0, keepdims=True))
                    dweight = right_product(values, dh)
                    total = jnp.sum(weight * dweight, axis=0, keepdims=True)
                    dscore = (weight * (dweight - total)).astype(jnp.bfloat16)
                    pk = jnp.dot(dscore, qh, preferred_element_type=f32)
                    pv = jnp.dot(weight.astype(jnp.bfloat16), dh, preferred_element_type=f32)
                    dk = pk if dk is None else dk + pk
                    dv = pv if dv is None else dv + pv
                if blocks == 1:
                    out_a[:, :, out_cols] = dk.astype(jnp.bfloat16).reshape(n, tokens, LANES)
                    out_b[:, :, out_cols] = dv.astype(jnp.bfloat16).reshape(n, tokens, LANES)
                else:
                    acc_a[...] += dk
                    acc_b[...] += dv

            if blocks == 1:
                block(0)
            else:
                pl.loop(0, blocks)(block)
                out_a[:, :, out_cols] = acc_a[...].astype(jnp.bfloat16).reshape(n, tokens, LANES)
                out_b[:, :, out_cols] = acc_b[...].astype(jnp.bfloat16).reshape(n, tokens, LANES)

        @pl.when(jnp.logical_not(encoder))
        def _():
            keys, values = cut(other, 0, c, every), cut(other, 1, c, every)

            def block(b):
                at = pl.ds(b * group, group)
                query, dout = cut(own, 0, c, at), cut(own, 1, c, at)
                ids = id_col[at, :, :].reshape(group * tokens, 1)
                mask = None
                dq, att = None, None
                for h in range(LANES // HEAD_DIM):
                    kh = jnp.where(lane == h, keys, zero)
                    vh = jnp.where(lane == h, values, zero)
                    score = right_product(query, kh)
                    if mask is None:
                        span = group * tokens
                        mask = jnp.concatenate(
                            [ids == id_row[i] for i in range(rows // span)], axis=1
                        )
                    expo = jnp.exp(jnp.where(mask, score, -jnp.inf))
                    weight = expo * (1.0 / jnp.sum(expo, axis=1, keepdims=True))
                    dweight = right_product(dout, vh)
                    total = jnp.sum(weight * dweight, axis=1, keepdims=True)
                    dscore = (weight * (dweight - total)).astype(jnp.bfloat16)
                    pq = jnp.dot(dscore, kh, preferred_element_type=f32)
                    pa = jnp.dot(weight.astype(jnp.bfloat16), vh, preferred_element_type=f32)
                    dq = pq if dq is None else dq + pq
                    att = pa if att is None else att + pa
                shape = (group, tokens, LANES)
                out_a[at, :, out_cols] = dq.astype(jnp.bfloat16).reshape(shape)
                out_b[at, :, out_cols] = att.astype(jnp.bfloat16).reshape(shape)

            if blocks == 1:
                block(0)
            else:
                pl.loop(0, blocks)(block)


def forward_kernel(
    n, m, group, normed, second, id_col, id_row, proj_a, proj_b,
    out_a, out_b, mine_a, mine_b,
    wbuf, paired, own, other, acc_a, acc_b, wsem,
    line_send, line_recv, sec_send, sec_recv, za_send, za_recv, mp_send, mp_recv, loc_sem,
):
    me = lax.axis_index("dp")
    col = lax.axis_index("mp")
    sec = lax.axis_index("section")
    tokens, width = normed.shape
    pieces = wbuf.shape[1]
    half = wbuf.shape[3]
    part = tokens // m
    cols = width // n

    def weight_copy(which, p):
        src = (proj_a, proj_b)[which]
        return pltpu.make_async_copy(
            src.at[0, :, pl.ds(p * half, half)], wbuf.at[which, p], wsem.at[which, p]
        )

    for p in range(pieces):
        for which in (0, 1):
            weight_copy(which, p).start()

    barrier = pltpu.get_barrier_semaphore()
    for j in range(1, n):
        pl.semaphore_signal(
            barrier, inc=1, device_id={"dp": lax.rem(me + j, n)}, device_id_type=MESH
        )
    for j in range(1, m):
        pl.semaphore_signal(
            barrier, inc=1, device_id={"mp": lax.rem(col + j, m)}, device_id_type=MESH
        )
    pl.semaphore_signal(barrier, inc=1, device_id={"section": 1 - sec}, device_id_type=MESH)
    pl.semaphore_wait(barrier, n + m - 1)

    band = pl.ds(pl.multiple_of(col * part, part), part)

    def line_copy(way, s, p):
        chunk = me - s if way == 0 else me + s
        target = me + 1 if way == 0 else me - 1
        src = paired.at[p] if s == 0 else own.at[p, chunk]
        return pltpu.make_async_remote_copy(
            src_ref=src, dst_ref=own.at[p, chunk],
            send_sem=line_send.at[way, s, p], recv_sem=line_recv.at[way, s, p],
            device_id={"dp": target}, device_id_type=MESH,
        )

    def line_ok(way, s):
        if way == 0:
            return jnp.logical_and(me - s >= 0, me < n - 1)
        return jnp.logical_and(me + s <= n - 1, me > 0)

    def got(way, s):
        return me - 1 - s >= 0 if way == 0 else me + 1 + s <= n - 1

    def sec_copy(chunk, p, src):
        return pltpu.make_async_remote_copy(
            src_ref=src, dst_ref=other.at[p, chunk],
            send_sem=sec_send.at[chunk, p], recv_sem=sec_recv.at[chunk, p],
            device_id={"section": 1 - sec}, device_id_type=MESH,
        )

    def za_copy(which, j):
        src, dst = ((normed, mine_a), (second, mine_b))[which]
        peer = lax.rem(me + j, n)
        return pltpu.make_async_remote_copy(
            src_ref=src.at[band, pl.ds(pl.multiple_of(peer * cols, cols), cols)],
            dst_ref=dst.at[me, band, :],
            send_sem=za_send.at[which, j], recv_sem=za_recv.at[which, j],
            device_id={"dp": peer}, device_id_type=MESH,
        )

    def mp_copy(which, j):
        dst = (mine_a, mine_b)[which]
        return pltpu.make_async_remote_copy(
            src_ref=dst.at[:, band, :], dst_ref=dst.at[:, band, :],
            send_sem=mp_send.at[which, j], recv_sem=mp_recv.at[which, j],
            device_id={"mp": lax.rem(col + j, m)}, device_id_type=MESH,
        )

    def local(which):
        src, dst = ((normed, mine_a), (second, mine_b))[which]
        return pltpu.make_async_copy(
            src.at[band, pl.ds(pl.multiple_of(me * cols, cols), cols)],
            dst.at[me, band, :], loc_sem.at[which],
        )

    def keep(p):
        return pltpu.make_async_copy(paired.at[p], own.at[p, me], loc_sem.at[2 + p])

    def second_too(fn):
        fn(0)
        pl.when(sec == 1)(lambda: fn(1))

    for j in range(1, n):
        second_too(lambda which: za_copy(which, j).start())
    second_too(lambda which: local(which).start())

    for p in range(pieces):
        for which in (0, 1):
            weight_copy(which, p).wait()
            rows_in = (normed, second)[which]
            paired[p, :, which * half : (which + 1) * half] = jnp.dot(
                rows_in[...], wbuf[which, p], preferred_element_type=jnp.float32
            ).astype(jnp.bfloat16)
        for way in (0, 1):
            pl.when(line_ok(way, 0))(lambda way=way, p=p: line_copy(way, 0, p).start())
        sec_copy(me, p, paired.at[p]).start()
        keep(p).start()

    def spread(which):
        local(which).wait()
        for j in range(1, n):
            za_copy(which, j).wait_recv()
        for j in range(1, m):
            mp_copy(which, j).start()

    second_too(spread)

    for wave in range(pieces + n - 2):
        for s in range(max(0, wave - pieces + 1), min(n - 1, wave + 1)):
            p = wave - s
            for way in (0, 1):

                @pl.when(got(way, s))
                def _():
                    line_copy(way, s, p).wait_recv()
                    chunk = me - 1 - s if way == 0 else me + 1 + s
                    if s + 1 < n - 1:
                        pl.when(line_ok(way, s + 1))(
                            lambda: line_copy(way, s + 1, p).start()
                        )
                    sec_copy(chunk, p, own.at[p, chunk]).start()

        p = wave - (n - 2)
        if p >= 0:
            keep(p).wait()
            for c in range(n):
                sec_copy(c, p, own.at[p, c]).wait_recv()
            attend_piece(
                sec == 0, p, group, id_col, id_row, own, other, out_a, out_b, acc_a, acc_b
            )

    def finish(which):
        for j in range(1, n):
            za_copy(which, j).wait_send()
        for j in range(1, m):
            mp_copy(which, j).wait()

    second_too(finish)
    for p in range(pieces):
        for s in range(n - 1):
            for way in (0, 1):
                pl.when(line_ok(way, s))(
                    lambda way=way, s=s, p=p: line_copy(way, s, p).wait_send()
                )
        for c in range(n):
            sec_copy(c, p, own.at[p, c]).wait_send()


def forward(n, m, normed, second, id_c, id_r, proj_a, proj_b):
    tokens, width = normed.shape
    inner = proj_a.shape[2]
    half = 2 * LANES
    pieces = inner // half
    rows = n * tokens
    group = max(1, min(n, 512 * 512 // (rows * tokens)))
    blocks = n // group
    grad = jax.ShapeDtypeStruct((n, tokens, inner), jnp.bfloat16)
    mine = jax.ShapeDtypeStruct((n, tokens, width // n), jnp.bfloat16)
    acc = (rows, LANES) if blocks > 1 else (8, LANES)
    dma = pltpu.SemaphoreType.DMA
    vmem = pl.BlockSpec(memory_space=pltpu.VMEM)
    anyw = pl.BlockSpec(memory_space=pltpu.HBM)
    bf16 = jnp.bfloat16
    return pl.pallas_call(
        functools.partial(forward_kernel, n, m, group),
        out_shape=(grad, grad, mine, mine),
        in_specs=[vmem] * 4 + [anyw] * 2,
        out_specs=[vmem, vmem, anyw, anyw],
        scratch_shapes=[
            pltpu.VMEM((2, pieces, width, half), bf16),
            pltpu.VMEM((pieces, tokens, 2 * half), bf16),
            pltpu.VMEM((pieces, n, tokens, 2 * half), bf16),
            pltpu.VMEM((pieces, n, tokens, 2 * half), bf16),
            pltpu.VMEM(acc, jnp.float32), pltpu.VMEM(acc, jnp.float32),
            dma((2, pieces)),
            dma((2, n, pieces)), dma((2, n, pieces)), dma((n, pieces)), dma((n, pieces)),
            dma((2, n)), dma((2, n)), dma((2, m)), dma((2, m)), dma((2 + pieces,)),
        ],
        compiler_params=pltpu.CompilerParams(
            collective_id=0, has_side_effects=True, vmem_limit_bytes=67000000
        ),
        name="forward",
    )(normed, second, id_c.reshape(n, tokens, 1), id_r.reshape(blocks, 1, rows // blocks),
      proj_a, proj_b)


def reduce_kernel(
    m, grad_a, grad_b, proj_a, proj_b, x_ref, gain_ref, result,
    left, wbuf, total, mine, partial, landed, gsem, wsem, send, recv,
):
    me = lax.axis_index("dp")
    col = lax.axis_index("mp")
    encoder = lax.axis_index("section") == 0
    tokens = x_ref.shape[0]
    part = tokens // m
    chunks, step = wbuf.shape[1:3]

    def left_copy(which):
        return pltpu.make_async_copy(
            (grad_a, grad_b)[which].at[me], left.at[which], gsem.at[which]
        )

    def weight_copy(which, c):
        return pltpu.make_async_copy(
            (proj_a, proj_b)[which].at[0, pl.ds(c * step, step), :],
            wbuf.at[which, c], wsem.at[which, c],
        )

    left_copy(0).start()
    pl.when(encoder)(lambda: left_copy(1).start())
    for c in range(chunks):
        weight_copy(0, c).start()
        pl.when(encoder)(lambda c=c: weight_copy(1, c).start())

    barrier = pltpu.get_barrier_semaphore()
    for j in range(1, m):
        pl.semaphore_signal(
            barrier, inc=1, device_id={"mp": lax.rem(col + j, m)}, device_id_type=MESH
        )
    pl.semaphore_wait(barrier, m - 1)

    def scatter(j, c):
        peer = lax.rem(col + j, m)
        rows = pl.ds(pl.multiple_of(peer * part, part), part)
        at = pl.ds(c * step, step)
        return pltpu.make_async_remote_copy(
            src_ref=partial.at[rows, at], dst_ref=landed.at[j, :, at],
            send_sem=send.at[j, c], recv_sem=recv.at[j, c],
            device_id={"mp": peer}, device_id_type=MESH,
        )

    band = pl.ds(pl.multiple_of(col * part, part), part)
    left_copy(0).wait()
    pl.when(encoder)(lambda: left_copy(1).wait())
    for c in range(chunks):
        weight_copy(0, c).wait()
        total[...] = right_product(left[0], wbuf[0, c])

        @pl.when(encoder)
        def _():
            weight_copy(1, c).wait()
            total[...] += right_product(left[1], wbuf[1, c])

        partial[:, c * step : (c + 1) * step] = total[...].astype(jnp.bfloat16)
        mine[:, c * step : (c + 1) * step] = total[band, :]
        for j in range(1, m):
            scatter(j, c).start()
    x = x_ref[band, :].astype(jnp.float32)
    scale = lax.rsqrt(jnp.mean(x * x, axis=-1, keepdims=True) + EPS)
    for j in range(1, m):
        for c in range(chunks):
            scatter(j, c).wait_recv()
    dnorm = mine[...]
    for j in range(1, m):
        dnorm = dnorm + landed[j].astype(jnp.float32)
    upper = gain_ref[...] * dnorm
    inner = jnp.mean(x * upper, axis=-1, keepdims=True)
    result[...] = (scale * upper - x * scale * scale * scale * inner).astype(jnp.bfloat16)
    for j in range(1, m):
        for c in range(chunks):
            scatter(j, c).wait_send()


def reduce_norm(m, grad_a, grad_b, proj_a, proj_b, states, gain):
    tokens, width = states.shape
    inner = proj_a.shape[2]
    part = tokens // m
    step = 4 * LANES
    chunks = width // step
    dma = pltpu.SemaphoreType.DMA
    bf16, f32 = jnp.bfloat16, jnp.float32
    vmem = pl.BlockSpec(memory_space=pltpu.VMEM)
    return pl.pallas_call(
        functools.partial(reduce_kernel, m),
        out_shape=jax.ShapeDtypeStruct((part, width), bf16),
        in_specs=[pl.BlockSpec(memory_space=pltpu.HBM)] * 4 + [vmem] * 2,
        out_specs=vmem,
        scratch_shapes=[
            pltpu.VMEM((2, tokens, inner), bf16),
            pltpu.VMEM((2, chunks, step, inner), bf16),
            pltpu.VMEM((tokens, step), f32),
            pltpu.VMEM((part, width), f32),
            pltpu.VMEM((tokens, width), bf16),
            pltpu.VMEM((m, part, width), bf16),
            dma((2,)), dma((2, chunks)), dma((m, chunks)), dma((m, chunks)),
        ],
        compiler_params=pltpu.CompilerParams(
            collective_id=1, has_side_effects=True, vmem_limit_bytes=66500000
        ),
        name="reduce_norm",
    )(grad_a, grad_b, proj_a, proj_b, states, gain)


def per_device(states, gains, proj_a, proj_b, cotangent, src_len, tgt_len, dest):
    encoder = lax.axis_index("section") == 0
    member = lax.axis_index("dp")
    n = lax.axis_size("dp")
    m = lax.axis_size("mp")
    gain = gains[0]
    weight_a = proj_a[0]
    weight_b = proj_b[0]
    tokens = states.shape[1]
    _, _, normed = rms_forward(states[0], gain)
    second_left = jnp.where(encoder, normed, cotangent)
    rows = n * tokens
    seqs = tgt_len.shape[1]
    names = jnp.arange(n * seqs, dtype=jnp.int32).reshape(n, seqs)
    id_c = sequence_of(
        jnp.where(encoder, src_len, tgt_len), jnp.where(encoder, dest, names), tokens
    )
    id_r = sequence_of(
        jnp.where(encoder, tgt_len, src_len), jnp.where(encoder, names, dest), tokens
    )
    grad_first, grad_second, mine_a, mine_b = forward(
        n, m, normed, second_left, id_c, id_r, proj_a, proj_b
    )
    mine = reduce_norm(m, grad_first, grad_second, proj_a, proj_b, states[0], gains)
    col = lax.axis_index("mp")
    landed = [mine] + [
        lax.ppermute(mine, "mp", [(i, (i + j) % m) for i in range(m)]) for j in range(1, m)
    ]
    mine_a = mine_a.reshape(rows, -1)
    mine_b = jnp.where(encoder, mine_a, mine_b.reshape(rows, -1))
    grad_a = left_product(mine_a, grad_first.reshape(rows, -1))
    grad_b = left_product(mine_b, grad_second.reshape(rows, -1))
    bands = []
    for b in range(m):
        band = landed[0]
        for j in range(1, m):
            band = jnp.where(col == (b + j) % m, landed[j], band)
        bands.append(band)
    grad_states = jnp.concatenate(bands, axis=0)
    return (grad_states[None], grad_a[None], grad_b[None])


def solution(mesh):
    return jax.shard_map(
        per_device,
        mesh=mesh,
        in_specs=(
            P("section", "dp", None),
            P("section", None),
            P("section", None, "mp"),
            P("section", None, "mp"),
            P("dp", None),
            P(),
            P(),
            P(),
        ),
        out_specs=(P("section", "dp", None), P("section", "dp", "mp"), P("section", "dp", "mp")),
        check_vma=False,
    )
```

profile of v0, /device:TPU:0, one launch (start us, length us, event | category | flops | bytes accessed | tf_op | source)
XLA Modules:
  0.0 100.4 jit_solution(17203409865168713758)
XLA Ops:
  0.6 0.0 copy-start
  0.7 1.6 %fusion = f32[128]{0:T(128)S(1)} fusion(bf16[1,128,4096]{2,1,0:T(8,128)(2,1)} %param.8), kind=kLoop, calls=%fused_computation.4 | loop fusion | flops 1572736 | bytes 1049088 | tf_op jit(solution)/shard_map/reduce_sum | solution.py:18
  2.3 0.7 fusion.11
  3.0 0.1 select_reduce_fusion.1
  3.1 0.1 select_reduce_fusion.2
  3.2 0.9 copy.16.id_col
  4.1 0.7 select_reduce_fusion
  4.8 0.0 copy-done
  4.8 2.6 %broadcast_select_fusion = (bf16[128,4096]{1,0:T(8,128)(2,1)}, bf16[128,4096]{1,0:T(8,128)(2,1)}) fusion(bf16[128,4096]{1,0:T(8,128)(2,1)} %param.12, pred[]{:T(512)S(6)} %eq.11, f32[4096]{0:T(1024)} %bitcast.19, f32[128]{0:T(128)S(1)} %add_rsqrt_fusion, bf16[1,128,4096]{2,1,0:T(8,128)(2,1)S(1)} %copy-done), kind=kLoop, calls=%fused_computation.10 | loop fusion | flops 2621440 | bytes 4211201 | tf_op jit(solution)/shard_map/jit(_where)/select_n | solution.py:456
  7.4 58.8 %forward.1 = (bf16[4,128,1024]{2,1,0:T(8,128)(2,1)}, bf16[4,128,1024]{2,1,0:T(8,128)(2,1)}, bf16[4,128,1024]{2,1,0:T(8,128)(2,1)}, bf16[4,128,1024]{2,1,0:T(8,128)(2,1)}) custom-call(bf16[128,4096]{1,0:T(8,128)(2,1)} %get-tuple-element.14.normed, bf16[128,4096]{1,0:T(8,128)(2,1)} %get-tuple-element.13.second, s32[4,128,1]{2,1,0:T(8,128)} %copy.16.id_col, ...), custom_call_target="tpu_custom_call" | custom-call | tf_op jit(solution)/shard_map/forward/pallas_call | solution.py:316
  66.2 20.5 %reduce_norm.1 = bf16[32,4096]{1,0:T(8,128)(2,1)} custom-call(bf16[4,128,1024]{2,1,0:T(8,128)(2,1)} %get-tuple-element.7.grad_a, bf16[4,128,1024]{2,1,0:T(8,128)(2,1)} %get-tuple-element.8.grad_b, bf16[1,4096,1024]{2,1,0:T(8,128)(2,1)} %proj_a.3, bf16[1,4096,1024]{2,1,0:T(8,128)(2,1)} %proj_b.3, bf16[128,4096]{1,0:T(8,128)(2,1)} %bitcast.18, f32[1,4096]{1,0:T(1,128)} %gain_ref.1), custom_call_target="tpu_custom_call" | custom-call | tf_op jit(solution)/shard_map/reduce_norm/pallas_call | solution.py:425
  86.7 1.4 %collective-permute-start.2 = (bf16[32,4096]{1,0:T(8,128)(2,1)}, bf16[32,4096]{1,0:T(8,128)(2,1)S(1)}, u32[]{:S(2)}, u32[]{:S(2)}) collective-permute-start(bf16[32,4096]{1,0:T(8,128)(2,1)} %reduce_norm.1), channel_id=1, source_target_pairs={{0,1},{1,2},{2,3},{3,0},{4,5},{5,6},{6,7},{7,4},{8,9},{9,10},{10,1... | collective-permute-start | bytes 786440 | tf_op jit(solution)/shard_map/ppermute | solution.py:472
  88.0 1.4 %collective-permute-start.1 = (bf16[32,4096]{1,0:T(8,128)(2,1)}, bf16[32,4096]{1,0:T(8,128)(2,1)S(1)}, u32[]{:S(2)}, u32[]{:S(2)}) collective-permute-start(bf16[32,4096]{1,0:T(8,128)(2,1)} %reduce_norm.1), channel_id=1, source_target_pairs={{0,2},{1,3},{2,0},{3,1},{4,6},{5,7},{6,4},{7,5},{8,10},{9,11},{10,... | collective-permute-start | bytes 786440 | tf_op jit(solution)/shard_map/ppermute | solution.py:472
  89.4 1.5 %collective-permute-start = (bf16[32,4096]{1,0:T(8,128)(2,1)}, bf16[32,4096]{1,0:T(8,128)(2,1)S(1)}, u32[]{:S(2)}, u32[]{:S(2)}) collective-permute-start(bf16[32,4096]{1,0:T(8,128)(2,1)} %reduce_norm.1), channel_id=1, source_target_pairs={{0,3},{1,0},{2,1},{3,2},{4,7},{5,4},{6,5},{7,6},{8,11},{9,8},{10,9... | collective-permute-start | bytes 786440 | tf_op jit(solution)/shard_map/ppermute | solution.py:472
  90.9 5.0 %convolution_bitcast_fusion = f32[1,1024,1024]{2,1,0:T(8,128)} fusion(bf16[4,128,1024]{2,1,0:T(8,128)(2,1)} %get-tuple-element.8.grad_b, bf16[4,128,1024]{2,1,0:T(8,128)(2,1)} %get-tuple-element.9, bf16[4,128,1024]{2,1,0:T(8,128)(2,1)} %get-tuple-element.10, pred[]{:T(512)S(6)} %eq.11), kind=kOutput, calls=%fused_computation.2 | convolution fusion | flops 1074266112 | bytes 7340033 | tf_op jit(solution)/shard_map/dot_general | solution.py:23
  95.9 0.0 copy-done.1
  95.9 0.0 copy-done.2
  95.9 3.3 %convolution_bitcast_fusion.1 = f32[1,1024,1024]{2,1,0:T(8,128)} fusion(bf16[4,128,1024]{2,1,0:T(8,128)(2,1)S(1)} %copy-done.1, bf16[4,128,1024]{2,1,0:T(8,128)(2,1)S(1)} %copy-done.2), kind=kOutput, calls=%fused_computation.3 | convolution fusion | flops 1073741824 | bytes 6291456 | tf_op jit(solution)/shard_map/dot_general | solution.py:23
  99.2 0.0 collective-permute-done.2
  99.2 0.0 collective-permute-done.1
  99.2 0.0 collective-permute-done
  99.2 0.0 copy-done.3
  99.2 0.1 select_select_fusion.3
  99.4 1.0 %maximum_bitcast_fusion = bf16[1,128,4096]{2,1,0:T(8,128)(2,1)} fusion(bf16[32,4096]{1,0:T(8,128)(2,1)S(1)} %get-tuple-element.16, bf16[32,4096]{1,0:T(8,128)(2,1)S(1)} %get-tuple-element.17, bf16[32,4096]{1,0:T(8,128)(2,1)S(1)} %get-tuple-element.18, bf16[32,4096]{1,0:T(8,128)(2,1)S(1)} %get-tuple-element.15), kind=kLoop, calls=%fused_computation.7 | loop fusion | flops 4194304 | bytes 2097152 | tf_op jit(solution)/shard_map/broadcast_in_dim | solution.py:485
  (5 shorter events, 0.0 us)
Async XLA Ops:
  0.6 4.1 %copy-start = (bf16[1,128,4096]{2,1,0:T(8,128)(2,1)S(1)}, bf16[1,128,4096]{2,1,0:T(8,128)(2,1)}, u32[]{:S(2)}) copy-start(bf16[1,128,4096]{2,1,0:T(8,128)(2,1)} %param.8) | copy-start | bytes 3145732
  86.7 12.6 %collective-permute-start.2 = (bf16[32,4096]{1,0:T(8,128)(2,1)}, bf16[32,4096]{1,0:T(8,128)(2,1)S(1)}, u32[]{:S(2)}, u32[]{:S(2)}) collective-permute-start(bf16[32,4096]{1,0:T(8,128)(2,1)} %reduce_norm.1), channel_id=1, source_target_pairs={{0,1},{1,2},{2,3},{3,0},{4,5},{5,6},{6,7},{7,4},{8,9},{9,10},{10,1... | collective-permute-start | bytes 786440 | tf_op jit(solution)/shard_map/ppermute | solution.py:472
  88.0 11.2 %collective-permute-start.1 = (bf16[32,4096]{1,0:T(8,128)(2,1)}, bf16[32,4096]{1,0:T(8,128)(2,1)S(1)}, u32[]{:S(2)}, u32[]{:S(2)}) collective-permute-start(bf16[32,4096]{1,0:T(8,128)(2,1)} %reduce_norm.1), channel_id=1, source_target_pairs={{0,2},{1,3},{2,0},{3,1},{4,6},{5,7},{6,4},{7,5},{8,10},{9,11},{10,... | collective-permute-start | bytes 786440 | tf_op jit(solution)/shard_map/ppermute | solution.py:472
  89.4 9.8 %collective-permute-start = (bf16[32,4096]{1,0:T(8,128)(2,1)}, bf16[32,4096]{1,0:T(8,128)(2,1)S(1)}, u32[]{:S(2)}, u32[]{:S(2)}) collective-permute-start(bf16[32,4096]{1,0:T(8,128)(2,1)} %reduce_norm.1), channel_id=1, source_target_pairs={{0,3},{1,0},{2,1},{3,2},{4,7},{5,4},{6,5},{7,6},{8,11},{9,8},{10,9... | collective-permute-start | bytes 786440 | tf_op jit(solution)/shard_map/ppermute | solution.py:472
  90.9 5.0 %copy-start.1 = (bf16[4,128,1024]{2,1,0:T(8,128)(2,1)S(1)}, bf16[4,128,1024]{2,1,0:T(8,128)(2,1)}, u32[]{:S(2)}) copy-start(bf16[4,128,1024]{2,1,0:T(8,128)(2,1)} %get-tuple-element.9) | copy-start | bytes 3145732
  90.9 5.0 %copy-start.2 = (bf16[4,128,1024]{2,1,0:T(8,128)(2,1)S(1)}, bf16[4,128,1024]{2,1,0:T(8,128)(2,1)}, u32[]{:S(2)}) copy-start(bf16[4,128,1024]{2,1,0:T(8,128)(2,1)} %get-tuple-element.7.grad_a) | copy-start | bytes 3145732
  95.9 3.3 %copy-start.3 = (bf16[32,4096]{1,0:T(8,128)(2,1)S(1)}, bf16[32,4096]{1,0:T(8,128)(2,1)}, u32[]{:S(2)}) copy-start(bf16[32,4096]{1,0:T(8,128)(2,1)} %reduce_norm.1) | copy-start | bytes 786436
where the time goes:
time: 101 us; the launch traced here: 100 us
  Pallas kernels  79.3 us (79%)
  matrix products  8.32 us (8%)
  other arithmetic  6.99 us (7%)
  starting transfers between devices  4.22 us (4%)
    pallas_call x1, Pallas kernels, forward(): pl.pallas_call(functools.partial(forward_kernel, n, m, group), out_shape=...  58.8 us
    pallas_call x1, Pallas kernels, reduce_norm(): pl.pallas_call(functools.partial(reduce_kernel, m), out_shape=jax.ShapeDt...  20.5 us
    dot_general x2, matrix products, left_product(): lax.dot_general(left, right, (((0,), (0,)), ((), ())), preferred_element_...  8.32 us
    ppermute x3, starting transfers between devices, per_device(): lax.ppermute(mine, 'mp', [(i, (i + j) % m) for i in range(m)])  4.22 us
    select_n x1, other arithmetic, per_device(): second_left = jnp.where(encoder, normed, cotangent)  2.6 us
  transfers between devices with their start and end apart: 3, of which 0 were waited for; matrix products, arithmetic and copies ran while one was open for 8% of the time, Pallas kernels for 0%

commit v1 on v0

--- a/solution.py
+++ b/solution.py
@@ -443,7 +443,7 @@
     )(grad_a, grad_b, proj_a, proj_b, states, gain)
 
 
-def per_device(states, gains, proj_a, proj_b, cotangent, src_len, tgt_len, dest):
+def stepwise(states, gains, proj_a, proj_b, cotangent, src_len, tgt_len, dest):
     encoder = lax.axis_index("section") == 0
     member = lax.axis_index("dp")
     n = lax.axis_size("dp")
@@ -485,6 +485,502 @@
     return (grad_states[None], grad_a[None], grad_b[None])
 
 
+def packed_ids(lengths, names, tokens):
+    n, seqs = lengths.shape
+    place = lax.broadcasted_iota(jnp.int32, (n, tokens), 1)
+    start = jnp.zeros((n, 1), jnp.int32)
+    ids = jnp.zeros((n, tokens), jnp.int32)
+    for i in range(seqs):
+        length = lengths[:, i : i + 1]
+        offset = place - start
+        ids = jnp.where((offset >= 0) & (offset < length), names(i), ids)
+        start = start + length
+    return ids.astype(jnp.float32)
+
+
+def fused_kernel(
+    n, m, x_hbm, cot_hbm, gain, src_len, tgt_len, dest, proj_a, proj_b,
+    result, out_a, out_b, mine_a, mine_b,
+    x, xall, wbuf, own, other, grad_a, grad_b, id_col, id_row, total, mine, partial, landed,
+    in_sem, wsem, loc_sem, out_sem, zx_send, zx_recv, px_send, px_recv, line_send, line_recv,
+    sec_send, sec_recv, za_send, za_recv, sl_send, sl_recv, rs_send, rs_recv, ag_send, ag_recv,
+):
+    me = lax.axis_index("dp")
+    col = lax.axis_index("mp")
+    sec = lax.axis_index("section")
+    encoder = sec == 0
+    decoder = sec == 1
+    tokens, width = x.shape
+    pieces, half = wbuf.shape[1], wbuf.shape[3]
+    part = tokens // m
+    cols = width // n
+    rows = n * tokens
+    step = total.shape[1]
+    chunks = width // step
+    seqs = src_len.shape[1]
+    f32, bf16 = jnp.float32, jnp.bfloat16
+    spare = lax.rem(me + 1, n)
+    near_x = col + 1 - 2 * lax.rem(col, 2)
+    near_y = lax.rem(col + 2, m)
+    band = pl.ds(pl.multiple_of(col * part, part), part)
+    lane = lax.broadcasted_iota(jnp.int32, (1, LANES), 1) // HEAD_DIM
+    zero = jnp.zeros((), bf16)
+
+    def remote(src, dst, send, recv, **device):
+        return pltpu.make_async_remote_copy(
+            src_ref=src, dst_ref=dst, send_sem=send, recv_sem=recv,
+            device_id=device, device_id_type=MESH,
+        )
+
+    def weight_copy(which, p):
+        src = (proj_a, proj_b)[which]
+        return pltpu.make_async_copy(
+            src.at[0, :, pl.ds(pl.multiple_of(p * half, half), half)],
+            wbuf.at[which, p], wsem.at[which, p],
+        )
+
+    x_copy = pltpu.make_async_copy(x_hbm.at[0], x, in_sem.at[0])
+    cot_copy = pltpu.make_async_copy(cot_hbm, xall.at[spare], in_sem.at[1])
+    x_copy.start()
+    pl.when(decoder)(cot_copy.start)
+    for p in range(pieces):
+        for which in (0, 1):
+            weight_copy(which, p).start()
+
+    barrier = pltpu.get_barrier_semaphore()
+    for j in range(1, n):
+        pl.semaphore_signal(
+            barrier, inc=1, device_id={"dp": lax.rem(me + j, n)}, device_id_type=MESH
+        )
+    for j in range(1, m):
+        pl.semaphore_signal(
+            barrier, inc=1, device_id={"mp": lax.rem(col + j, m)}, device_id_type=MESH
+        )
+    pl.semaphore_signal(barrier, inc=1, device_id={"section": 1 - sec}, device_id_type=MESH)
+    pl.semaphore_wait(barrier, n + m - 1)
+
+    def source(way, s):
+        return me - (1 - 2 * way) * (1 + s)
+
+    def got(way, s):
+        src = source(way, s)
+        return jnp.logical_and(src >= 0, src < n)
+
+    def line_ok(way, s):
+        chunk = source(way, s - 1)
+        target = me + 1 - 2 * way
+        inside = jnp.logical_and(chunk >= 0, chunk < n)
+        return jnp.logical_and(inside, jnp.logical_and(target >= 0, target < n))
+
+    def zx_copy(way, s):
+        ref = xall.at[source(way, s - 1), band, :]
+        return remote(ref, ref, zx_send.at[way, s], zx_recv.at[way, s], dp=me + 1 - 2 * way)
+
+    def line_copy(way, s, p):
+        ref = own.at[p, source(way, s - 1)]
+        return remote(
+            ref, ref, line_send.at[way, s, p], line_recv.at[way, s, p], dp=me + 1 - 2 * way
+        )
+
+    def sec_copy(chunk, p):
+        return remote(
+            own.at[p, chunk], other.at[p, chunk],
+            sec_send.at[chunk, p], sec_recv.at[chunk, p], section=1 - sec,
+        )
+
+    def plane(view, send, recv, kind):
+        small = part // 2
+        start = (col * part, col * part, near_x * part, near_y * part + small)[kind]
+        size = (part, part, small, small)[kind]
+        target = (near_x, near_y, near_y, near_x)[kind]
+        ref = view(pl.ds(pl.multiple_of(start, small), size))
+        return remote(ref, ref, send.at[kind], recv.at[kind], mp=target)
+
+    def px_copy(src, kind):
+        return plane(
+            lambda at: xall.at[src, at, :], px_send.at[src], px_recv.at[src], kind
+        )
+
+    def za_copy(which, j):
+        peer = lax.rem(me + j, n)
+        src = xall.at[(me, spare)[which]]
+        return remote(
+            src.at[band, pl.ds(pl.multiple_of(peer * cols, cols), cols)],
+            (mine_a, mine_b)[which].at[me, band, :],
+            za_send.at[which, j], za_recv.at[which, j], dp=peer,
+        )
+
+    def sl_copy(which, j, kind):
+        block = lax.rem(me + n - j, n)
+        return plane(
+            lambda at: (mine_a, mine_b)[which].at[block, at, :],
+            sl_send.at[which, j], sl_recv.at[which, j], kind,
+        )
+
+    def scatter(j, d):
+        peer = lax.rem(col + j, m)
+        at = pl.ds(pl.multiple_of(d * step, step), step)
+        return remote(
+            partial.at[pl.ds(pl.multiple_of(peer * part, part), part), at],
+            landed.at[j, :, at], rs_send.at[j, d], rs_recv.at[j, d], mp=peer,
+        )
+
+    def gather(j):
+        return remote(
+            result.at[band, :], result.at[band, :],
+            ag_send.at[j], ag_recv.at[j], mp=lax.rem(col + j, m),
+        )
+
+    my_cols = pl.ds(pl.multiple_of(me * cols, cols), cols)
+
+    def keep_slice(which):
+        src = xall.at[(me, spare)[which]]
+        return pltpu.make_async_copy(
+            src.at[:, my_cols], (mine_a, mine_b)[which].at[me], loc_sem.at[which]
+        )
+
+    def keep_all(which):
+        return pltpu.make_async_copy(
+            xall.at[:, :, my_cols], (mine_a, mine_b)[which], loc_sem.at[which]
+        )
+
+    def grad_out(which):
+        return pltpu.make_async_copy(
+            (grad_a, grad_b)[which], (out_a, out_b)[which], out_sem.at[which]
+        )
+
+    @pl.when(decoder)
+    def _():
+        cot_copy.wait()
+        for j in range(1, n):
+            za_copy(1, j).start()
+        keep_slice(1).start()
+
+    x_copy.wait()
+    group = min(tokens, 16)
+
+    @pl.loop(0, tokens // group)
+    def _(r):
+        at = pl.ds(pl.multiple_of(r * group, group), group)
+        xf = x[at, :].astype(f32)
+        scale = lax.rsqrt(jnp.mean(xf * xf, axis=-1, keepdims=True) + EPS)
+        xall[me, at, :] = (xf * scale * gain[...]).astype(bf16)
+
+    @pl.when(encoder)
+    def _():
+        for way in (0, 1):
+            pl.when(line_ok(way, 0))(lambda way=way: zx_copy(way, 0).start())
+
+    @pl.when(decoder)
+    def _():
+        for j in range(1, n):
+            za_copy(0, j).start()
+        keep_slice(0).start()
+
+    src_ids = packed_ids(src_len, lambda i: dest[:, i : i + 1], tokens)
+    device = lax.broadcasted_iota(jnp.int32, (n, 1), 0)
+    tgt_ids = packed_ids(tgt_len, lambda i: device * seqs + i, tokens)
+    id_row[...] = jnp.where(encoder, tgt_ids, src_ids)
+    near_ids = jnp.where(encoder, src_ids, tgt_ids)
+    for b in range(n):
+        id_col[b] = jnp.transpose(jnp.broadcast_to(near_ids[b : b + 1, :], (LANES, tokens)))
+
+    def project(p, blk_a, blk_b, out):
+        for which in (0, 1):
+            own[p, out, :, which * half : (which + 1) * half] = jnp.dot(
+                xall[(blk_a, blk_b)[which]], wbuf[which, p], preferred_element_type=f32
+            ).astype(bf16)
+        sec_copy(out, p).start()
+
+    def x_line(s):
+        for way in (0, 1):
+
+            @pl.when(got(way, s))
+            def _():
+                zx_copy(way, s).wait_recv()
+                pl.when(line_ok(way, s + 1))(lambda: zx_copy(way, s + 1).start())
+                px_copy(source(way, s), 0).start()
+                px_copy(source(way, s), 1).start()
+
+    def x_near(s):
+        for way in (0, 1):
+
+            @pl.when(got(way, s))
+            def _():
+                src = source(way, s)
+                px_copy(src, 0).wait_recv()
+                px_copy(src, 2).start()
+                px_copy(src, 1).wait_recv()
+                px_copy(src, 3).start()
+
+    @pl.loop(0, pieces)
+    def _(p):
+        for which in (0, 1):
+            weight_copy(which, p).wait()
+        project(p, me, lax.rem(me + sec, n), me)
+
+        @pl.when(decoder)
+        def _():
+            for way in (0, 1):
+                pl.when(line_ok(way, 0))(lambda way=way: line_copy(way, 0, p).start())
+
+        pl.when(jnp.logical_and(encoder, p == pieces // 2))(lambda: x_line(0))
+
+    def unit(axis, p, blk):
+        @pl.loop(0, half // LANES)
+        def _(c):
+            lo = pl.ds(pl.multiple_of(c * LANES, LANES), LANES)
+            hi = pl.ds(pl.multiple_of(half + c * LANES, LANES), LANES)
+            at = pl.ds(pl.multiple_of(p * half + c * LANES, LANES), LANES)
+            near_a, near_b = own[p, blk, :, lo], own[p, blk, :, hi]
+            far_a = other[p, :, :, lo].reshape(rows, LANES)
+            far_b = other[p, :, :, hi].reshape(rows, LANES)
+            ids = id_col[blk]
+            mask = jnp.concatenate([ids == id_row[b : b + 1, :] for b in range(n)], axis=1)
+            sum_a, sum_b = None, None
+            for h in range(LANES // HEAD_DIM):
+                fa = jnp.where(lane == h, far_a, zero)
+                fb = jnp.where(lane == h, far_b, zero)
+                expo = jnp.exp(jnp.where(mask, right_product(near_a, fa), -jnp.inf))
+                norm = jnp.sum(expo, axis=axis, keepdims=True)
+                weight = expo * (1.0 / jnp.where(norm == 0.0, 1.0, norm))
+                dweight = right_product(near_b, fb)
+                shift = jnp.sum(weight * dweight, axis=axis, keepdims=True)
+                dscore = (weight * (dweight - shift)).astype(bf16)
+                pa = jnp.dot(dscore, fa, preferred_element_type=f32)
+                pb = jnp.dot(weight.astype(bf16), fb, preferred_element_type=f32)
+                sum_a = pa if sum_a is None else sum_a + pa
+                sum_b = pb if sum_b is None else sum_b + pb
+            grad_a[blk, :, at] = sum_a.astype(bf16)
+            grad_b[blk, :, at] = sum_b.astype(bf16)
+
+    def others(axis, p):
+        @pl.loop(1, n)
+        def _(j):
+            unit(axis, p, lax.rem(me + j, n))
+
+    def ready(p):
+        for c in range(n):
+            sec_copy(c, p).wait_recv()
+
+    def reduce_own(which_all):
+        @pl.loop(0, chunks)
+        def _(d):
+            at = pl.ds(pl.multiple_of(d * step, step), step)
+            acc = None
+            for which in which_all:
+                for p in range(pieces):
+                    left = (grad_a, grad_b)[which][me, :, p * half : (p + 1) * half]
+                    term = right_product(left, wbuf[which, p, at, :])
+                    acc = term if acc is None else acc + term
+            total[...] = acc
+            partial[:, at] = acc.astype(bf16)
+            mine[:, at] = total[band, :]
+            for j in range(1, m):
+                scatter(j, d).start()
+
+    def finish_own():
+        xf = x[band, :].astype(f32)
+        scale = lax.rsqrt(jnp.mean(xf * xf, axis=-1, keepdims=True) + EPS)
+        for j in range(1, m):
+            for d in range(chunks):
+                scatter(j, d).wait_recv()
+        dnorm = mine[...]
+        for j in range(1, m):
+            dnorm = dnorm + landed[j].astype(f32)
+        upper = gain[...] * dnorm
+        inner = jnp.mean(xf * upper, axis=-1, keepdims=True)
+        result[band, :] = (scale * upper - xf * scale * scale * scale * inner).astype(bf16)
+        for j in range(1, m):
+            gather(j).start()
+
+    def wave(w):
+        for s in range(max(0, w - pieces + 1), min(n - 1, w + 1)):
+            p = w - s
+            for way in (0, 1):
+
+                @pl.when(got(way, s))
+                def _():
+                    line_copy(way, s, p).wait_recv()
+                    if s + 1 < n - 1:
+                        pl.when(line_ok(way, s + 1))(
+                            lambda: line_copy(way, s + 1, p).start()
+                        )
+                    sec_copy(source(way, s), p).start()
+
+    @pl.when(encoder)
+    def _():
+        @pl.loop(0, n)
+        def _(t):
+            pl.when(t < n - 2)(lambda: x_line(t + 1))
+            pl.when(t < n - 1)(lambda: x_near(t))
+
+            @pl.when(t >= 1)
+            def _():
+                @pl.loop(0, 2)
+                def _(way):
+                    @pl.when(got(way, t - 1))
+                    def _():
+                        src = source(way, t - 1)
+                        px_copy(src, 2).wait_recv()
+                        px_copy(src, 3).wait_recv()
+                        pl.loop(0, pieces)(lambda p: project(p, src, src, src))
+
+        for which in (0, 1):
+            keep_all(which).start()
+
+        @pl.loop(0, pieces)
+        def _(p):
+            ready(p)
+            unit(0, p, me)
+            pl.when(jnp.logical_and(p >= 1, p < pieces - 1))(lambda: others(0, p - 1))
+
+        reduce_own((0, 1))
+        pl.loop(pieces - 2, pieces)(lambda p: others(0, p))
+        for which in (0, 1):
+            grad_out(which).start()
+        finish_own()
+        for way in (0, 1):
+            for s in range(n - 1):
+                pl.when(line_ok(way, s))(lambda way=way, s=s: zx_copy(way, s).wait_send())
+
+                @pl.when(got(way, s))
+                def _():
+                    for kind in range(4):
+                        px_copy(source(way, s), kind).wait_send()
+        for which in (0, 1):
+            keep_all(which).wait()
+
+    @pl.when(decoder)
+    def _():
+        for w in range(pieces):
+            wave(w)
+        for which in (0, 1):
+            for j in range(1, n):
+                za_copy(which, j).wait_recv()
+                for kind in (0, 1):
+                    sl_copy(which, j, kind).start()
+
+        @pl.loop(0, pieces)
+        def _(p):
+            ready(p)
+            unit(1, p, me)
+
+        reduce_own((0,))
+        for which in (0, 1):
+            for j in range(1, n):
+                for kind in (0, 1):
+                    sl_copy(which, j, kind).wait_recv()
+                    sl_copy(which, j, 2 + kind).start()
+        for w in range(pieces, pieces + n - 2):
+            wave(w)
+
+        @pl.loop(0, pieces)
+        def _(p):
+            others(1, p)
+            pl.when(p == 1)(finish_own)
+
+        for which in (0, 1):
+            grad_out(which).start()
+        for which in (0, 1):
+            keep_slice(which).wait()
+            for j in range(1, n):
+                za_copy(which, j).wait_send()
+                for kind in range(4):
+                    sl_copy(which, j, kind).wait_send()
+                for kind in (2, 3):
+                    sl_copy(which, j, kind).wait_recv()
+        for p in range(pieces):
+            for s in range(n - 1):
+                for way in (0, 1):
+                    pl.when(line_ok(way, s))(
+                        lambda way=way, s=s, p=p: line_copy(way, s, p).wait_send()
+                    )
+
+    for p in range(pieces):
+        for c in range(n):
+            sec_copy(c, p).wait_send()
+    for j in range(1, m):
+        for d in range(chunks):
+            scatter(j, d).wait_send()
+        gather(j).wait()
+    for which in (0, 1):
+        grad_out(which).wait()
+
+
+def fused_scratch(n, m, tokens, width, inner, half, step):
+    pieces = inner // half
+    part = tokens // m
+    chunks = width // step
+    dma = pltpu.SemaphoreType.DMA
+    vmem = pltpu.VMEM
+    bf16, f32 = jnp.bfloat16, jnp.float32
+    buffers = [
+        vmem((tokens, width), bf16), vmem((n, tokens, width), bf16),
+        vmem((2, pieces, width, half), bf16),
+        vmem((pieces, n, tokens, 2 * half), bf16), vmem((pieces, n, tokens, 2 * half), bf16),
+        vmem((n, tokens, inner), bf16), vmem((n, tokens, inner), bf16),
+        vmem((n, tokens, LANES), f32), vmem((n, tokens), f32),
+        vmem((tokens, step), f32), vmem((part, width), f32),
+        vmem((tokens, width), bf16), vmem((m, part, width), bf16),
+    ]
+    pair = lambda *shape: [dma(shape), dma(shape)]
+    sems = [dma((2,)), dma((2, pieces)), dma((2,)), dma((2,))]
+    sems += pair(2, n) + pair(n, 4) + pair(2, n, pieces) + pair(n, pieces)
+    sems += pair(2, n) + pair(2, n, 4) + pair(m, chunks) + pair(m)
+    return buffers, sems
+
+
+def fused_fits(n, m, tokens, width, inner):
+    if m != 4 or n < 2 or tokens != LANES or inner < 4 * LANES:
+        return False
+    buffers, _ = fused_scratch(n, m, tokens, width, inner, 2 * LANES, 4 * LANES)
+    size = 0
+    for buffer in buffers:
+        count = jnp.dtype(buffer.dtype).itemsize
+        for extent in buffer.shape:
+            count *= extent
+        size += count
+    return size + tokens * width * 2 < 48 * 2**20
+
+
+def fused(n, m, states, gains, proj_a, proj_b, cotangent, src_len, tgt_len, dest):
+    _, tokens, width = states.shape
+    inner = proj_a.shape[2]
+    buffers, sems = fused_scratch(n, m, tokens, width, inner, 2 * LANES, 4 * LANES)
+    bf16 = jnp.bfloat16
+    grad = jax.ShapeDtypeStruct((n, tokens, inner), bf16)
+    slices = jax.ShapeDtypeStruct((n, tokens, width // n), bf16)
+    vmem = pl.BlockSpec(memory_space=pltpu.VMEM)
+    hbm = pl.BlockSpec(memory_space=pltpu.HBM)
+    return pl.pallas_call(
+        functools.partial(fused_kernel, n, m),
+        out_shape=(jax.ShapeDtypeStruct((tokens, width), bf16), grad, grad, slices, slices),
+        in_specs=[hbm, hbm, vmem, vmem, vmem, vmem, hbm, hbm],
+        out_specs=[vmem, hbm, hbm, hbm, hbm],
+        scratch_shapes=buffers + sems,
+        compiler_params=pltpu.CompilerParams(
+            collective_id=2, has_side_effects=True, vmem_limit_bytes=56 * 2**20
+        ),
+        name="fused",
+    )(states, cotangent, gains, src_len, tgt_len, dest, proj_a, proj_b)
+
+
+def per_device(states, gains, proj_a, proj_b, cotangent, src_len, tgt_len, dest):
+    n = lax.axis_size("dp")
+    m = lax.axis_size("mp")
+    _, tokens, width = states.shape
+    inner = proj_a.shape[2]
+    args = (states, gains, proj_a, proj_b, cotangent, src_len, tgt_len, dest)
+    if not fused_fits(n, m, tokens, width, inner):
+        return stepwise(*args)
+    result, grad_first, grad_second, mine_a, mine_b = fused(n, m, *args)
+    rows = n * tokens
+    grad_a = left_product(mine_a.reshape(rows, -1), grad_first.reshape(rows, -1))
+    grad_b = left_product(mine_b.reshape(rows, -1), grad_second.reshape(rows, -1))
+    return (result[None], grad_a[None], grad_b[None])
+
+
 def solution(mesh):
     return jax.shard_map(
         per_device,

time: 101 us -> 105 us (1.040)
  Pallas kernels: 79.3 us -> 95.4 us
  other arithmetic: 6.99 us -> 0 us
  starting transfers between devices: 4.22 us -> 0 us
    pallas_call x2 -> x1, Pallas kernels: 79.3 us -> 95.4 us  [fused(): pl.pallas_call(functools.partial(fused_kernel, n, m), out_shape=(jax.Shap...]
    ppermute x3 -> x0, starting transfers between devices: 4.22 us -> none  [per_device(): lax.ppermute(mine, 'mp', [(i, (i + j) % m) for i in range(m)])]
    select_n x3 -> x0, other arithmetic: 3.45 us -> none  [the longest x1 2.6 us: per_device(): second_left = jnp.where(encoder, normed, cotangent)]
    reduce_sum x4 -> x0, other arithmetic: 2.49 us -> none  [the longest x1 1.6 us: rms_forward(): scale = lax.rsqrt(jnp.mean(xf * xf, axis=-1, keepdims=True) + EPS)]
  transfers between devices with their start and end apart: 3 -> 0, of which waited for: 0 -> 0; matrix products, arithmetic and copies ran while one was open for 8% -> 0% of each run, Pallas kernels for 0% -> 0%
where the time goes in v1:
time: 105 us
  Pallas kernels  95.4 us (91%)
  matrix products  8.3 us (8%)
    pallas_call x1, Pallas kernels, fused(): pl.pallas_call(functools.partial(fused_kernel, n, m), out_shape=(jax.Shap...  95.4 us
    dot_general x2, matrix products, left_product(): lax.dot_general(left, right, (((0,), (0,)), ((), ())), preferred_element_...  8.3 us

profile of v1, /device:TPU:0, one launch (start us, length us, event | category | flops | bytes accessed | tf_op | source)
XLA Modules:
  0.0 105.3 jit_solution(3488582208476366166)
XLA Ops:
  0.6 95.4 %fused.1 = (bf16[128,4096]{1,0:T(8,128)(2,1)}, bf16[4,128,1024]{2,1,0:T(8,128)(2,1)}, bf16[4,128,1024]{2,1,0:T(8,128)(2,1)}, bf16[4,128,1024]{2,1,0:T(8,128)(2,1)}, bf16[4,128,1024]{2,1,0:T(8,128)(2,1)}) custom-call(bf16[1,128,4096]{2,1,0:T(8,128)(2,1)} %x_hbm.1, bf16[128,4096]{1,0:T(8,128)(2,1)} %cot_hbm.1, f32[1,4096]{1,0:T(1,128)} %gain.1, ...), custom_call_target="tpu_custom_call" | custom-call | tf_op jit(solution)/shard_map/fused/pallas_call | solution.py:956
  96.0 0.0 copy-start
  96.0 0.0 copy-start.2
  96.0 5.0 %convolution_bitcast_fusion.1 = f32[1,1024,1024]{2,1,0:T(8,128)} fusion(bf16[4,128,1024]{2,1,0:T(8,128)(2,1)} %get-tuple-element.9, bf16[4,128,1024]{2,1,0:T(8,128)(2,1)} %get-tuple-element.10), kind=kOutput, calls=%fused_computation.1 | convolution fusion | flops 1073741824 | bytes 6291456 | tf_op jit(solution)/shard_map/dot_general | solution.py:23
  101.0 0.0 copy-done
  101.0 0.0 copy-done.2
  101.0 0.0 copy-start.1
  101.0 3.3 %convolution_bitcast_fusion = f32[1,1024,1024]{2,1,0:T(8,128)} fusion(bf16[4,128,1024]{2,1,0:T(8,128)(2,1)S(1)} %copy-done, bf16[4,128,1024]{2,1,0:T(8,128)(2,1)S(1)} %copy-done.2), kind=kOutput, calls=%fused_computation | convolution fusion | flops 1073741824 | bytes 6291456 | tf_op jit(solution)/shard_map/dot_general | solution.py:23
  104.3 0.0 copy-done.1
  104.3 1.0 copy.16
Async XLA Ops:
  96.0 5.0 %copy-start = (bf16[4,128,1024]{2,1,0:T(8,128)(2,1)S(1)}, bf16[4,128,1024]{2,1,0:T(8,128)(2,1)}, u32[]{:S(2)}) copy-start(bf16[4,128,1024]{2,1,0:T(8,128)(2,1)} %get-tuple-element.11) | copy-start | bytes 3145732
  96.0 5.0 %copy-start.2 = (bf16[4,128,1024]{2,1,0:T(8,128)(2,1)S(1)}, bf16[4,128,1024]{2,1,0:T(8,128)(2,1)}, u32[]{:S(2)}) copy-start(bf16[4,128,1024]{2,1,0:T(8,128)(2,1)} %get-tuple-element.12) | copy-start | bytes 3145732
  101.0 3.3 %copy-start.1 = (bf16[128,4096]{1,0:T(8,128)(2,1)S(1)}, bf16[128,4096]{1,0:T(8,128)(2,1)}, u32[]{:S(2)}) copy-start(bf16[128,4096]{1,0:T(8,128)(2,1)} %get-tuple-element.8) | copy-start | bytes 3145732

commit v2 on v1

--- a/solution.py
+++ b/solution.py
@@ -499,10 +499,10 @@
 
 
 def fused_kernel(
-    n, m, x_hbm, cot_hbm, gain, src_len, tgt_len, dest, proj_a, proj_b,
+    n, m, x_hbm, cot_hbm, gain_hbm, src_hbm, tgt_hbm, dest_hbm, proj_a, proj_b,
     result, out_a, out_b, mine_a, mine_b,
-    x, xall, wbuf, own, other, grad_a, grad_b, id_col, id_row, total, mine, partial, landed,
-    in_sem, wsem, loc_sem, out_sem, zx_send, zx_recv, px_send, px_recv, line_send, line_recv,
+    gain, src_len, tgt_len, dest, rest, x, xall, wbuf, own, other, grad_a, grad_b, id_col, id_row, total, partial, landed,
+    gate, in_sem, wsem, loc_sem, out_sem, zx_send, zx_recv, px_send, px_recv, line_send, line_recv,
     sec_send, sec_recv, za_send, za_recv, sl_send, sl_recv, rs_send, rs_recv, ag_send, ag_recv,
 ):
     me = lax.axis_index("dp")
@@ -515,8 +515,10 @@
     part = tokens // m
     cols = width // n
     rows = n * tokens
-    step = total.shape[1]
-    chunks = width // step
+    chunks = rs_send.shape[1]
+    step = width // chunks
+    quarter = width // pieces
+    hops = (n - 1) * pieces
     seqs = src_len.shape[1]
     f32, bf16 = jnp.float32, jnp.bfloat16
     spare = lax.rem(me + 1, n)
@@ -541,7 +543,15 @@
 
     x_copy = pltpu.make_async_copy(x_hbm.at[0], x, in_sem.at[0])
     cot_copy = pltpu.make_async_copy(cot_hbm, xall.at[spare], in_sem.at[1])
+    small_copies = [
+        pltpu.make_async_copy(src, dst, in_sem.at[2 + i])
+        for i, (src, dst) in enumerate(
+            ((gain_hbm, gain), (src_hbm, src_len), (tgt_hbm, tgt_len), (dest_hbm, dest))
+        )
+    ]
     x_copy.start()
+    for copy in small_copies:
+        copy.start()
     pl.when(decoder)(cot_copy.start)
     for p in range(pieces):
         for which in (0, 1):
@@ -572,9 +582,14 @@
         inside = jnp.logical_and(chunk >= 0, chunk < n)
         return jnp.logical_and(inside, jnp.logical_and(target >= 0, target < n))
 
-    def zx_copy(way, s):
-        ref = xall.at[source(way, s - 1), band, :]
-        return remote(ref, ref, zx_send.at[way, s], zx_recv.at[way, s], dp=me + 1 - 2 * way)
+    def span(q):
+        return pl.ds(pl.multiple_of(q * quarter, quarter), quarter)
+
+    def zx_copy(way, s, q):
+        ref = xall.at[source(way, s - 1), band, span(q)]
+        return remote(
+            ref, ref, zx_send.at[way, s, q], zx_recv.at[way, s, q], dp=me + 1 - 2 * way
+        )
 
     def line_copy(way, s, p):
         ref = own.at[p, source(way, s - 1)]
@@ -596,9 +611,9 @@
         ref = view(pl.ds(pl.multiple_of(start, small), size))
         return remote(ref, ref, send.at[kind], recv.at[kind], mp=target)
 
-    def px_copy(src, kind):
+    def px_copy(src, q, kind):
         return plane(
-            lambda at: xall.at[src, at, :], px_send.at[src], px_recv.at[src], kind
+            lambda at: xall.at[src, at, span(q)], px_send.at[src, q], px_recv.at[src, q], kind
         )
 
     def za_copy(which, j):
@@ -625,11 +640,15 @@
             landed.at[j, :, at], rs_send.at[j, d], rs_recv.at[j, d], mp=peer,
         )
 
-    def gather(j):
+    def gather(kind):
+        if kind > 1:
+            return plane(lambda at: result.at[at, :], ag_send, ag_recv, kind)
         return remote(
-            result.at[band, :], result.at[band, :],
-            ag_send.at[j], ag_recv.at[j], mp=lax.rem(col + j, m),
-        )
+            rest, result.at[band, :], ag_send.at[kind], ag_recv.at[kind],
+            mp=(near_x, near_y)[kind],
+        )
+
+    keep_rest = pltpu.make_async_copy(rest, result.at[band, :], loc_sem.at[2])
 
     my_cols = pl.ds(pl.multiple_of(me * cols, cols), cols)
 
@@ -654,9 +673,10 @@
         cot_copy.wait()
         for j in range(1, n):
             za_copy(1, j).start()
-        keep_slice(1).start()
 
     x_copy.wait()
+    for copy in small_copies:
+        copy.wait()
     group = min(tokens, 16)
 
     @pl.loop(0, tokens // group)
@@ -668,14 +688,16 @@
 
     @pl.when(encoder)
     def _():
-        for way in (0, 1):
-            pl.when(line_ok(way, 0))(lambda way=way: zx_copy(way, 0).start())
+        for q in range(pieces):
+            for way in (0, 1):
+                pl.when(line_ok(way, 0))(lambda way=way, q=q: zx_copy(way, 0, q).start())
 
     @pl.when(decoder)
     def _():
         for j in range(1, n):
             za_copy(0, j).start()
-        keep_slice(0).start()
+        for which in (0, 1):
+            keep_slice(which).start()
 
     src_ids = packed_ids(src_len, lambda i: dest[:, i : i + 1], tokens)
     device = lax.broadcasted_iota(jnp.int32, (n, 1), 0)
@@ -692,26 +714,41 @@
             ).astype(bf16)
         sec_copy(out, p).start()
 
-    def x_line(s):
+    def x_line(i):
+        s, q = i // pieces, i % pieces
         for way in (0, 1):
 
             @pl.when(got(way, s))
             def _():
-                zx_copy(way, s).wait_recv()
-                pl.when(line_ok(way, s + 1))(lambda: zx_copy(way, s + 1).start())
-                px_copy(source(way, s), 0).start()
-                px_copy(source(way, s), 1).start()
-
-    def x_near(s):
+                zx_copy(way, s, q).wait_recv()
+                pl.when(line_ok(way, s + 1))(lambda: zx_copy(way, s + 1, q).start())
+                for kind in (0, 1):
+                    px_copy(source(way, s), q, kind).start()
+
+    def x_near(i):
+        s, q = i // pieces, i % pieces
         for way in (0, 1):
 
             @pl.when(got(way, s))
             def _():
-                src = source(way, s)
-                px_copy(src, 0).wait_recv()
-                px_copy(src, 2).start()
-                px_copy(src, 1).wait_recv()
-                px_copy(src, 3).start()
+                for kind in (0, 1):
+                    px_copy(source(way, s), q, kind).wait_recv()
+                    px_copy(source(way, s), q, 2 + kind).start()
+
+    def x_done(i):
+        s, q = i // pieces, i % pieces
+        for way in (0, 1):
+
+            @pl.when(got(way, s))
+            def _():
+                for kind in (2, 3):
+                    px_copy(source(way, s), q, kind).wait_recv()
+
+    def x_work(i):
+        @pl.loop(0, 2)
+        def _(way):
+            src = source(way, i // pieces)
+            pl.when(got(way, i // pieces))(lambda: project(i % pieces, src, src, src))
 
     @pl.loop(0, pieces)
     def _(p):
@@ -719,15 +756,8 @@
             weight_copy(which, p).wait()
         project(p, me, lax.rem(me + sec, n), me)
 
-        @pl.when(decoder)
-        def _():
-            for way in (0, 1):
-                pl.when(line_ok(way, 0))(lambda way=way: line_copy(way, 0, p).start())
-
-        pl.when(jnp.logical_and(encoder, p == pieces // 2))(lambda: x_line(0))
-
     def unit(axis, p, blk):
-        @pl.loop(0, half // LANES)
+        @pl.loop(0, half // LANES, unroll=True)
         def _(c):
             lo = pl.ds(pl.multiple_of(c * LANES, LANES), LANES)
             hi = pl.ds(pl.multiple_of(half + c * LANES, LANES), LANES)
@@ -764,7 +794,7 @@
             sec_copy(c, p).wait_recv()
 
     def reduce_own(which_all):
-        @pl.loop(0, chunks)
+        @pl.loop(0, chunks, unroll=2)
         def _(d):
             at = pl.ds(pl.multiple_of(d * step, step), step)
             acc = None
@@ -773,9 +803,8 @@
                     left = (grad_a, grad_b)[which][me, :, p * half : (p + 1) * half]
                     term = right_product(left, wbuf[which, p, at, :])
                     acc = term if acc is None else acc + term
-            total[...] = acc
+            total[:, at] = acc
             partial[:, at] = acc.astype(bf16)
-            mine[:, at] = total[band, :]
             for j in range(1, m):
                 scatter(j, d).start()
 
@@ -785,14 +814,20 @@
         for j in range(1, m):
             for d in range(chunks):
                 scatter(j, d).wait_recv()
-        dnorm = mine[...]
+        dnorm = total[band, :]
         for j in range(1, m):
             dnorm = dnorm + landed[j].astype(f32)
         upper = gain[...] * dnorm
         inner = jnp.mean(xf * upper, axis=-1, keepdims=True)
-        result[band, :] = (scale * upper - xf * scale * scale * scale * inner).astype(bf16)
-        for j in range(1, m):
-            gather(j).start()
+        rest[...] = (scale * upper - xf * scale * scale * scale * inner).astype(bf16)
+        gather(0).start()
+        gather(1).start()
+        keep_rest.start()
+
+    def relay_own():
+        for kind in (0, 1):
+            gather(kind).wait_recv()
+            gather(2 + kind).start()
 
     def wave(w):
         for s in range(max(0, w - pieces + 1), min(n - 1, w + 1)):
@@ -810,21 +845,20 @@
 
     @pl.when(encoder)
     def _():
-        @pl.loop(0, n)
-        def _(t):
-            pl.when(t < n - 2)(lambda: x_line(t + 1))
-            pl.when(t < n - 1)(lambda: x_near(t))
-
-            @pl.when(t >= 1)
+        lags = (0, 2, 5, 4 + pieces)
+
+        @pl.loop(0, hops + lags[3])
+        def _(i):
+            for lag, stage in zip(lags, (x_line, x_near, x_done, x_work)):
+                at = i - lag
+                inside = jnp.logical_and(at >= 0, at < hops)
+                pl.when(inside)(lambda stage=stage, at=at: stage(at))
+
+            @pl.when(i == pieces - 1)
             def _():
-                @pl.loop(0, 2)
-                def _(way):
-                    @pl.when(got(way, t - 1))
-                    def _():
-                        src = source(way, t - 1)
-                        px_copy(src, 2).wait_recv()
-                        px_copy(src, 3).wait_recv()
-                        pl.loop(0, pieces)(lambda p: project(p, src, src, src))
+                pl.semaphore_signal(
+                    gate, inc=1, device_id={"section": 1 - sec}, device_id_type=MESH
+                )
 
         for which in (0, 1):
             keep_all(which).start()
@@ -833,26 +867,40 @@
         def _(p):
             ready(p)
             unit(0, p, me)
-            pl.when(jnp.logical_and(p >= 1, p < pieces - 1))(lambda: others(0, p - 1))
 
         reduce_own((0, 1))
-        pl.loop(pieces - 2, pieces)(lambda p: others(0, p))
+
+        @pl.loop(0, pieces)
+        def _(p):
+            others(0, p)
+            pl.when(p == 1)(finish_own)
+            pl.when(p == 2)(relay_own)
+
         for which in (0, 1):
             grad_out(which).start()
-        finish_own()
-        for way in (0, 1):
-            for s in range(n - 1):
-                pl.when(line_ok(way, s))(lambda way=way, s=s: zx_copy(way, s).wait_send())
+
+        @pl.loop(0, hops)
+        def _(i):
+            s, q = i // pieces, i % pieces
+            for way in (0, 1):
+                pl.when(line_ok(way, s))(lambda way=way: zx_copy(way, s, q).wait_send())
 
                 @pl.when(got(way, s))
                 def _():
                     for kind in range(4):
-                        px_copy(source(way, s), kind).wait_send()
+                        px_copy(source(way, s), q, kind).wait_send()
+
         for which in (0, 1):
             keep_all(which).wait()
 
     @pl.when(decoder)
     def _():
+        pl.semaphore_wait(gate, 1)
+        for p in range(pieces):
+            for way in (0, 1):
+                pl.when(line_ok(way, 0))(
+                    lambda way=way, p=p: line_copy(way, 0, p).start()
+                )
         for w in range(pieces):
             wave(w)
         for which in (0, 1):
@@ -865,6 +913,8 @@
         def _(p):
             ready(p)
             unit(1, p, me)
+            for late in range(n - 2):
+                pl.when(p == min(late, pieces - 1))(lambda late=late: wave(pieces + late))
 
         reduce_own((0,))
         for which in (0, 1):
@@ -872,13 +922,11 @@
                 for kind in (0, 1):
                     sl_copy(which, j, kind).wait_recv()
                     sl_copy(which, j, 2 + kind).start()
-        for w in range(pieces, pieces + n - 2):
-            wave(w)
-
         @pl.loop(0, pieces)
         def _(p):
             others(1, p)
             pl.when(p == 1)(finish_own)
+            pl.when(p == 2)(relay_own)
 
         for which in (0, 1):
             grad_out(which).start()
@@ -903,12 +951,16 @@
     for j in range(1, m):
         for d in range(chunks):
             scatter(j, d).wait_send()
-        gather(j).wait()
+    for kind in range(4):
+        gather(kind).wait_send()
+    for kind in (2, 3):
+        gather(kind).wait_recv()
+    keep_rest.wait()
     for which in (0, 1):
         grad_out(which).wait()
 
 
-def fused_scratch(n, m, tokens, width, inner, half, step):
+def fused_scratch(n, m, seqs, tokens, width, inner, half, step):
     pieces = inner // half
     part = tokens // m
     chunks = width // step
@@ -916,25 +968,26 @@
     vmem = pltpu.VMEM
     bf16, f32 = jnp.bfloat16, jnp.float32
     buffers = [
+        vmem((1, width), f32), vmem((n, seqs), jnp.int32), vmem((n, seqs), jnp.int32),
+        vmem((n, seqs), jnp.int32), vmem((part, width), bf16),
         vmem((tokens, width), bf16), vmem((n, tokens, width), bf16),
         vmem((2, pieces, width, half), bf16),
         vmem((pieces, n, tokens, 2 * half), bf16), vmem((pieces, n, tokens, 2 * half), bf16),
         vmem((n, tokens, inner), bf16), vmem((n, tokens, inner), bf16),
         vmem((n, tokens, LANES), f32), vmem((n, tokens), f32),
-        vmem((tokens, step), f32), vmem((part, width), f32),
-        vmem((tokens, width), bf16), vmem((m, part, width), bf16),
+        vmem((tokens, width), f32), vmem((tokens, width), bf16), vmem((m, part, width), bf16),
     ]
     pair = lambda *shape: [dma(shape), dma(shape)]
-    sems = [dma((2,)), dma((2, pieces)), dma((2,)), dma((2,))]
-    sems += pair(2, n) + pair(n, 4) + pair(2, n, pieces) + pair(n, pieces)
-    sems += pair(2, n) + pair(2, n, 4) + pair(m, chunks) + pair(m)
+    sems = [pltpu.SemaphoreType.REGULAR, dma((6,)), dma((2, pieces)), dma((3,)), dma((2,))]
+    sems += pair(2, n, pieces) + pair(n, pieces, 4) + pair(2, n, pieces) + pair(n, pieces)
+    sems += pair(2, n) + pair(2, n, 4) + pair(m, chunks) + pair(4)
     return buffers, sems
 
 
-def fused_fits(n, m, tokens, width, inner):
+def fused_fits(n, m, seqs, tokens, width, inner):
     if m != 4 or n < 2 or tokens != LANES or inner < 4 * LANES:
         return False
-    buffers, _ = fused_scratch(n, m, tokens, width, inner, 2 * LANES, 4 * LANES)
+    buffers, _ = fused_scratch(n, m, seqs, tokens, width, inner, 2 * LANES, 4 * LANES)
     size = 0
     for buffer in buffers:
         count = jnp.dtype(buffer.dtype).itemsize
@@ -947,17 +1000,16 @@
 def fused(n, m, states, gains, proj_a, proj_b, cotangent, src_len, tgt_len, dest):
     _, tokens, width = states.shape
     inner = proj_a.shape[2]
-    buffers, sems = fused_scratch(n, m, tokens, width, inner, 2 * LANES, 4 * LANES)
+    buffers, sems = fused_scratch(n, m, src_len.shape[1], tokens, width, inner, 2 * LANES, 4 * LANES)
     bf16 = jnp.bfloat16
     grad = jax.ShapeDtypeStruct((n, tokens, inner), bf16)
     slices = jax.ShapeDtypeStruct((n, tokens, width // n), bf16)
-    vmem = pl.BlockSpec(memory_space=pltpu.VMEM)
     hbm = pl.BlockSpec(memory_space=pltpu.HBM)
     return pl.pallas_call(
         functools.partial(fused_kernel, n, m),
         out_shape=(jax.ShapeDtypeStruct((tokens, width), bf16), grad, grad, slices, slices),
-        in_specs=[hbm, hbm, vmem, vmem, vmem, vmem, hbm, hbm],
-        out_specs=[vmem, hbm, hbm, hbm, hbm],
+        in_specs=[hbm] * 8,
+        out_specs=[hbm] * 5,
         scratch_shapes=buffers + sems,
         compiler_params=pltpu.CompilerParams(
             collective_id=2, has_side_effects=True, vmem_limit_bytes=56 * 2**20
@@ -966,19 +1018,89 @@
     )(states, cotangent, gains, src_len, tgt_len, dest, proj_a, proj_b)
 
 
+def grads_kernel(
+    left_a, left_b, right_a, right_b, states_in, out_a, out_b, states_out,
+    left, right, states, out, left_sem, right_sem, states_sem, out_sem,
+):
+    tiles, tile = out.shape[1:3]
+    loads = []
+    for which, (src_left, src_right) in enumerate(((left_a, right_a), (left_b, right_b))):
+        loads.append((
+            pltpu.make_async_copy(src_right, right.at[which], right_sem.at[which]),
+            pltpu.make_async_copy(src_left, left.at[which], left_sem.at[which]),
+        ))
+    for pair in loads:
+        for copy in pair:
+            copy.start()
+    bring = pltpu.make_async_copy(states_in, states, states_sem.at[0])
+    give = pltpu.make_async_copy(states, states_out.at[0], states_sem.at[1])
+    bring.start()
+
+    def store(which, t):
+        at = pl.ds(pl.multiple_of(t * tile, tile), tile)
+        return pltpu.make_async_copy(
+            out.at[which, t], (out_a, out_b)[which].at[0, at, :], out_sem.at[which, t]
+        )
+
+    for which in (0, 1):
+        for copy in loads[which]:
+            copy.wait()
+        for t in range(tiles):
+            part = left[which, :, t * tile : (t + 1) * tile]
+            out[which, t] = left_product(part, right[which])
+            store(which, t).start()
+        if which == 0:
+            bring.wait()
+            give.start()
+    for which in (0, 1):
+        for t in range(tiles):
+            store(which, t).wait()
+    give.wait()
+
+
+def grads(left_a, left_b, right_a, right_b, states):
+    rows, cols = left_a.shape
+    inner = right_a.shape[1]
+    tokens, width = states.shape
+    tile = min(cols, 2 * LANES)
+    tiles = cols // tile
+    bf16, f32 = jnp.bfloat16, jnp.float32
+    dma = pltpu.SemaphoreType.DMA
+    hbm = pl.BlockSpec(memory_space=pltpu.HBM)
+    return pl.pallas_call(
+        grads_kernel,
+        out_shape=(
+            jax.ShapeDtypeStruct((1, cols, inner), f32),
+            jax.ShapeDtypeStruct((1, cols, inner), f32),
+            jax.ShapeDtypeStruct((1, tokens, width), bf16),
+        ),
+        in_specs=[hbm] * 5,
+        out_specs=[hbm] * 3,
+        scratch_shapes=[
+            pltpu.VMEM((2, rows, cols), bf16), pltpu.VMEM((2, rows, inner), bf16),
+            pltpu.VMEM((tokens, width), bf16), pltpu.VMEM((2, tiles, tile, inner), f32),
+            dma((2,)), dma((2,)), dma((2,)), dma((2, tiles)),
+        ],
+        compiler_params=pltpu.CompilerParams(vmem_limit_bytes=62 * 2**20),
+        name="grads",
+    )(left_a, left_b, right_a, right_b, states)
+
+
 def per_device(states, gains, proj_a, proj_b, cotangent, src_len, tgt_len, dest):
     n = lax.axis_size("dp")
     m = lax.axis_size("mp")
     _, tokens, width = states.shape
     inner = proj_a.shape[2]
     args = (states, gains, proj_a, proj_b, cotangent, src_len, tgt_len, dest)
-    if not fused_fits(n, m, tokens, width, inner):
+    if not fused_fits(n, m, src_len.shape[1], tokens, width, inner):
         return stepwise(*args)
     result, grad_first, grad_second, mine_a, mine_b = fused(n, m, *args)
     rows = n * tokens
-    grad_a = left_product(mine_a.reshape(rows, -1), grad_first.reshape(rows, -1))
-    grad_b = left_product(mine_b.reshape(rows, -1), grad_second.reshape(rows, -1))
-    return (result[None], grad_a[None], grad_b[None])
+    grad_a, grad_b, grad_states = grads(
+        mine_a.reshape(rows, -1), mine_b.reshape(rows, -1),
+        grad_first.reshape(rows, -1), grad_second.reshape(rows, -1), result,
+    )
+    return (grad_states, grad_a, grad_b)
 
 
 def solution(mesh):

time: 105 us -> 82.7 us (0.79)
  Pallas kernels: 95.4 us -> 81.7 us
  matrix products: 8.3 us -> 0 us
    pallas_call x1, Pallas kernels: 95.4 us -> 76 us  [fused(): pl.pallas_call(functools.partial(fused_kernel, n, m), out_shape=(jax.Shap...]
    dot_general x2 -> x0, matrix products: 8.3 us -> none  [left_product(): lax.dot_general(left, right, (((0,), (0,)), ((), ())), preferred_element_...]
    pallas_call x0 -> x1, Pallas kernels: none -> 5.75 us  [grads(): pl.pallas_call(grads_kernel, out_shape=(jax.ShapeDtypeStruct((1, cols, in...]
where the time goes in v2:
time: 82.7 us; the launch traced here: 82.5 us
  Pallas kernels  81.7 us (99%)
    pallas_call x1, Pallas kernels, fused(): pl.pallas_call(functools.partial(fused_kernel, n, m), out_shape=(jax.Shap...  76 us
    pallas_call x1, Pallas kernels, grads(): pl.pallas_call(grads_kernel, out_shape=(jax.ShapeDtypeStruct((1, cols, in...  5.75 us

profile of v2, /device:TPU:0, one launch (start us, length us, event | category | flops | bytes accessed | tf_op | source)
XLA Modules:
  0.0 82.5 jit_solution(14977916243386250909)
XLA Ops:
  0.6 76.0 %fused.1 = (bf16[128,4096]{1,0:T(8,128)(2,1)}, bf16[4,128,1024]{2,1,0:T(8,128)(2,1)}, bf16[4,128,1024]{2,1,0:T(8,128)(2,1)}, bf16[4,128,1024]{2,1,0:T(8,128)(2,1)}, bf16[4,128,1024]{2,1,0:T(8,128)(2,1)}) custom-call(bf16[1,128,4096]{2,1,0:T(8,128)(2,1)} %x_hbm.1, bf16[128,4096]{1,0:T(8,128)(2,1)} %cot_hbm.1, f32[1,4096]{1,0:T(1,128)} %gain_hbm.1, ...), custom_call_target="tpu_custom_call" | custom-call | tf_op jit(solution)/shard_map/fused/pallas_call | solution.py:1008
  76.6 5.7 %grads.1 = (f32[1,1024,1024]{2,1,0:T(8,128)}, f32[1,1024,1024]{2,1,0:T(8,128)}, bf16[1,128,4096]{2,1,0:T(8,128)(2,1)}) custom-call(bf16[512,1024]{1,0:T(8,128)(2,1)} %bitcast.6, bf16[512,1024]{1,0:T(8,128)(2,1)} %bitcast.7, bf16[512,1024]{1,0:T(8,128)(2,1)} %bitcast.4, bf16[512,1024]{1,0:T(8,128)(2,1)} %bitcast.5, bf16[128,4096]{1,0:T(8,128)(2,1)} %get-tuple-element.15.states_in), custom_call_target="tpu_custom_call" | custom-call | tf_op jit(solution)/shard_map/grads/pallas_call | solution.py:1070

commit v3 on v2

--- a/solution.py
+++ b/solution.py
@@ -10,6 +10,7 @@
 HEAD_DIM = 64
 LANES = 128
 EPS = 1e-06
+MAX_LEN = 16
 MESH = pl.DeviceIdType.MESH
 
 
@@ -495,13 +496,13 @@
         offset = place - start
         ids = jnp.where((offset >= 0) & (offset < length), names(i), ids)
         start = start + length
-    return ids.astype(jnp.float32)
+    return (ids + 1).astype(jnp.float32)
 
 
 def fused_kernel(
     n, m, x_hbm, cot_hbm, gain_hbm, src_hbm, tgt_hbm, dest_hbm, proj_a, proj_b,
     result, out_a, out_b, mine_a, mine_b,
-    gain, src_len, tgt_len, dest, rest, x, xall, wbuf, own, other, grad_a, grad_b, id_col, id_row, total, partial, landed,
+    gain, src_len, tgt_len, dest, rest, x, xall, wbuf, own, other, grad_a, grad_b, id_col, id_row, pick, id_far, far, total, partial, landed,
     gate, in_sem, wsem, loc_sem, out_sem, zx_send, zx_recv, px_send, px_recv, line_send, line_recv,
     sec_send, sec_recv, za_send, za_recv, sl_send, sl_recv, rs_send, rs_recv, ag_send, ag_recv,
 ):
@@ -520,6 +521,7 @@
     quarter = width // pieces
     hops = (n - 1) * pieces
     seqs = src_len.shape[1]
+    cap = far.shape[0]
     f32, bf16 = jnp.float32, jnp.bfloat16
     spare = lax.rem(me + 1, n)
     near_x = col + 1 - 2 * lax.rem(col, 2)
@@ -567,6 +569,18 @@
             barrier, inc=1, device_id={"mp": lax.rem(col + j, m)}, device_id_type=MESH
         )
     pl.semaphore_signal(barrier, inc=1, device_id={"section": 1 - sec}, device_id_type=MESH)
+    x_copy.wait()
+    for copy in small_copies:
+        copy.wait()
+    group = min(tokens, 16)
+
+    @pl.loop(0, tokens // group)
+    def _(r):
+        at = pl.ds(pl.multiple_of(r * group, group), group)
+        xf = x[at, :].astype(f32)
+        scale = lax.rsqrt(jnp.mean(xf * xf, axis=-1, keepdims=True) + EPS)
+        xall[me, at, :] = (xf * scale * gain[...]).astype(bf16)
+
     pl.semaphore_wait(barrier, n + m - 1)
 
     def source(way, s):
@@ -663,9 +677,11 @@
             xall.at[:, :, my_cols], (mine_a, mine_b)[which], loc_sem.at[which]
         )
 
-    def grad_out(which):
+    def grad_out(which, p):
+        of = pl.ds(pl.multiple_of(p * half, half), half)
         return pltpu.make_async_copy(
-            (grad_a, grad_b)[which], (out_a, out_b)[which], out_sem.at[which]
+            (grad_a, grad_b)[which].at[:, :, of], (out_a, out_b)[which].at[:, :, of],
+            out_sem.at[which, p],
         )
 
     @pl.when(decoder)
@@ -673,18 +689,6 @@
         cot_copy.wait()
         for j in range(1, n):
             za_copy(1, j).start()
-
-    x_copy.wait()
-    for copy in small_copies:
-        copy.wait()
-    group = min(tokens, 16)
-
-    @pl.loop(0, tokens // group)
-    def _(r):
-        at = pl.ds(pl.multiple_of(r * group, group), group)
-        xf = x[at, :].astype(f32)
-        scale = lax.rsqrt(jnp.mean(xf * xf, axis=-1, keepdims=True) + EPS)
-        xall[me, at, :] = (xf * scale * gain[...]).astype(bf16)
 
     @pl.when(encoder)
     def _():
@@ -706,6 +710,29 @@
     near_ids = jnp.where(encoder, src_ids, tgt_ids)
     for b in range(n):
         id_col[b] = jnp.transpose(jnp.broadcast_to(near_ids[b : b + 1, :], (LANES, tokens)))
+    flat = jnp.concatenate([id_row[b : b + 1, :] for b in range(n)], axis=1)
+    flat = jnp.broadcast_to(flat, (16, rows)).astype(bf16)
+    before = lax.broadcasted_iota(jnp.int32, (rows, rows), 0)
+    before = before < lax.broadcasted_iota(jnp.int32, (rows, rows), 1)
+    before = jnp.where(before, 1.0, 0.0).astype(bf16)
+    slot = lax.broadcasted_iota(jnp.int32, (cap, rows), 0).astype(f32)
+    for b in range(n):
+        member = jnp.concatenate(
+            [
+                jnp.max(
+                    jnp.where(id_col[b] == id_row[c : c + 1, :], 1.0, 0.0), axis=0, keepdims=True
+                )
+                for c in range(n)
+            ],
+            axis=1,
+        )
+        rank = jnp.dot(
+            jnp.broadcast_to(member, (16, rows)).astype(bf16), before, preferred_element_type=f32
+        )[0:1, :]
+        key = jnp.where(member > 0.0, rank, -1.0)
+        chosen = jnp.where(key == slot, 1.0, 0.0).astype(bf16)
+        pick[b] = chosen
+        id_far[b] = right_product(flat, chosen)
 
     def project(p, blk_a, blk_b, out):
         for which in (0, 1):
@@ -756,33 +783,47 @@
             weight_copy(which, p).wait()
         project(p, me, lax.rem(me + sec, n), me)
 
+    heads = LANES // HEAD_DIM
+
+    def stack(near):
+        return jnp.concatenate([jnp.where(lane == h, near, zero) for h in range(heads)], axis=0)
+
+    def merge(left, right):
+        whole = jnp.dot(left.reshape(-1, cap), right, preferred_element_type=f32)
+        whole = whole.reshape(heads, tokens, LANES)
+        picked = whole[0]
+        for h in range(1, heads):
+            picked = jnp.where(lane == h, whole[h], picked)
+        return picked.astype(bf16)
+
     def unit(axis, p, blk):
+        far[...] = jnp.dot(
+            pick[blk], other[p].reshape(rows, 2 * half), preferred_element_type=f32
+        ).astype(bf16)
+        mask = jnp.concatenate(
+            [
+                id_col[blk] == id_far[blk, 0:1, c * LANES : (c + 1) * LANES]
+                for c in range(cap // LANES)
+            ],
+            axis=1,
+        )
+
         @pl.loop(0, half // LANES, unroll=True)
         def _(c):
             lo = pl.ds(pl.multiple_of(c * LANES, LANES), LANES)
             hi = pl.ds(pl.multiple_of(half + c * LANES, LANES), LANES)
             at = pl.ds(pl.multiple_of(p * half + c * LANES, LANES), LANES)
             near_a, near_b = own[p, blk, :, lo], own[p, blk, :, hi]
-            far_a = other[p, :, :, lo].reshape(rows, LANES)
-            far_b = other[p, :, :, hi].reshape(rows, LANES)
-            ids = id_col[blk]
-            mask = jnp.concatenate([ids == id_row[b : b + 1, :] for b in range(n)], axis=1)
-            sum_a, sum_b = None, None
-            for h in range(LANES // HEAD_DIM):
-                fa = jnp.where(lane == h, far_a, zero)
-                fb = jnp.where(lane == h, far_b, zero)
-                expo = jnp.exp(jnp.where(mask, right_product(near_a, fa), -jnp.inf))
-                norm = jnp.sum(expo, axis=axis, keepdims=True)
-                weight = expo * (1.0 / jnp.where(norm == 0.0, 1.0, norm))
-                dweight = right_product(near_b, fb)
-                shift = jnp.sum(weight * dweight, axis=axis, keepdims=True)
-                dscore = (weight * (dweight - shift)).astype(bf16)
-                pa = jnp.dot(dscore, fa, preferred_element_type=f32)
-                pb = jnp.dot(weight.astype(bf16), fb, preferred_element_type=f32)
-                sum_a = pa if sum_a is None else sum_a + pa
-                sum_b = pb if sum_b is None else sum_b + pb
-            grad_a[blk, :, at] = sum_a.astype(bf16)
-            grad_b[blk, :, at] = sum_b.astype(bf16)
+            far_a, far_b = far[:, lo], far[:, hi]
+            score = right_product(stack(near_a), far_a).reshape(heads, tokens, cap)
+            expo = jnp.exp(jnp.where(mask[None], score, -jnp.inf))
+            norm = jnp.sum(expo, axis=axis + 1, keepdims=True)
+            weight = expo * (1.0 / jnp.where(norm == 0.0, 1.0, norm))
+            dweight = right_product(stack(near_b), far_b).reshape(heads, tokens, cap)
+            shift = jnp.sum(weight * dweight, axis=axis + 1, keepdims=True)
+            dscore = (weight * (dweight - shift)).astype(bf16)
+            grad_a[blk, :, at] = merge(dscore, far_a)
+            grad_b[blk, :, at] = merge(weight.astype(bf16), far_b)
 
     def others(axis, p):
         @pl.loop(1, n)
@@ -854,7 +895,7 @@
                 inside = jnp.logical_and(at >= 0, at < hops)
                 pl.when(inside)(lambda stage=stage, at=at: stage(at))
 
-            @pl.when(i == pieces - 1)
+            @pl.when(i == 1)
             def _():
                 pl.semaphore_signal(
                     gate, inc=1, device_id={"section": 1 - sec}, device_id_type=MESH
@@ -873,11 +914,11 @@
         @pl.loop(0, pieces)
         def _(p):
             others(0, p)
+            for which in (0, 1):
+                grad_out(which, p).start()
             pl.when(p == 1)(finish_own)
             pl.when(p == 2)(relay_own)
 
-        for which in (0, 1):
-            grad_out(which).start()
 
         @pl.loop(0, hops)
         def _(i):
@@ -925,11 +966,11 @@
         @pl.loop(0, pieces)
         def _(p):
             others(1, p)
+            for which in (0, 1):
+                grad_out(which, p).start()
             pl.when(p == 1)(finish_own)
             pl.when(p == 2)(relay_own)
 
-        for which in (0, 1):
-            grad_out(which).start()
         for which in (0, 1):
             keep_slice(which).wait()
             for j in range(1, n):
@@ -957,12 +998,14 @@
         gather(kind).wait_recv()
     keep_rest.wait()
     for which in (0, 1):
-        grad_out(which).wait()
+        for p in range(pieces):
+            grad_out(which, p).wait()
 
 
 def fused_scratch(n, m, seqs, tokens, width, inner, half, step):
     pieces = inner // half
     part = tokens // m
+    cap = min(n * tokens, seqs * MAX_LEN)
     chunks = width // step
     dma = pltpu.SemaphoreType.DMA
     vmem = pltpu.VMEM
@@ -975,17 +1018,18 @@
         vmem((pieces, n, tokens, 2 * half), bf16), vmem((pieces, n, tokens, 2 * half), bf16),
         vmem((n, tokens, inner), bf16), vmem((n, tokens, inner), bf16),
         vmem((n, tokens, LANES), f32), vmem((n, tokens), f32),
+        vmem((n, cap, n * tokens), bf16), vmem((n, 16, cap), f32), vmem((cap, 2 * half), bf16),
         vmem((tokens, width), f32), vmem((tokens, width), bf16), vmem((m, part, width), bf16),
     ]
     pair = lambda *shape: [dma(shape), dma(shape)]
-    sems = [pltpu.SemaphoreType.REGULAR, dma((6,)), dma((2, pieces)), dma((3,)), dma((2,))]
+    sems = [pltpu.SemaphoreType.REGULAR, dma((6,)), dma((2, pieces)), dma((3,)), dma((2, pieces))]
     sems += pair(2, n, pieces) + pair(n, pieces, 4) + pair(2, n, pieces) + pair(n, pieces)
     sems += pair(2, n) + pair(2, n, 4) + pair(m, chunks) + pair(4)
     return buffers, sems
 
 
 def fused_fits(n, m, seqs, tokens, width, inner):
-    if m != 4 or n < 2 or tokens != LANES or inner < 4 * LANES:
+    if m != 4 or n < 2 or tokens != LANES or inner < 4 * LANES or n * seqs > 256:
         return False
     buffers, _ = fused_scratch(n, m, seqs, tokens, width, inner, 2 * LANES, 4 * LANES)
     size = 0

time: 82.7 us -> 80.2 us (0.970)
  Pallas kernels: 81.7 us -> 79.4 us
    pallas_call x1, Pallas kernels: 76 us -> 73.6 us  [fused(): pl.pallas_call(functools.partial(fused_kernel, n, m), out_shape=(jax.Shap...]
where the time goes in v3:
time: 80.2 us; the launch traced here: 80 us
  Pallas kernels  79.4 us (99%)
    pallas_call x1, Pallas kernels, fused(): pl.pallas_call(functools.partial(fused_kernel, n, m), out_shape=(jax.Shap...  73.6 us
    pallas_call x1, Pallas kernels, grads(): pl.pallas_call(grads_kernel, out_shape=(jax.ShapeDtypeStruct((1, cols, in...  5.74 us

profile of v3, /device:TPU:0, one launch (start us, length us, event | category | flops | bytes accessed | tf_op | source)
XLA Modules:
  0.0 80.0 jit_solution(5097364064159889268)
XLA Ops:
  0.6 73.6 %fused.1 = (bf16[128,4096]{1,0:T(8,128)(2,1)}, bf16[4,128,1024]{2,1,0:T(8,128)(2,1)}, bf16[4,128,1024]{2,1,0:T(8,128)(2,1)}, bf16[4,128,1024]{2,1,0:T(8,128)(2,1)}, bf16[4,128,1024]{2,1,0:T(8,128)(2,1)}) custom-call(bf16[1,128,4096]{2,1,0:T(8,128)(2,1)} %x_hbm.1, bf16[128,4096]{1,0:T(8,128)(2,1)} %cot_hbm.1, f32[1,4096]{1,0:T(1,128)} %gain_hbm.1, ...), custom_call_target="tpu_custom_call" | custom-call | tf_op jit(solution)/shard_map/fused/pallas_call | solution.py:1052
  74.3 5.7 %grads.1 = (f32[1,1024,1024]{2,1,0:T(8,128)}, f32[1,1024,1024]{2,1,0:T(8,128)}, bf16[1,128,4096]{2,1,0:T(8,128)(2,1)}) custom-call(bf16[512,1024]{1,0:T(8,128)(2,1)} %bitcast.6, bf16[512,1024]{1,0:T(8,128)(2,1)} %bitcast.7, bf16[512,1024]{1,0:T(8,128)(2,1)} %bitcast.4, bf16[512,1024]{1,0:T(8,128)(2,1)} %bitcast.5, bf16[128,4096]{1,0:T(8,128)(2,1)} %get-tuple-element.15.states_in), custom_call_target="tpu_custom_call" | custom-call | tf_op jit(solution)/shard_map/grads/pallas_call | solution.py:1114

commit v4 on v3

--- a/solution.py
+++ b/solution.py
@@ -516,8 +516,8 @@
     part = tokens // m
     cols = width // n
     rows = n * tokens
-    chunks = rs_send.shape[1]
-    step = width // chunks
+    step = 4 * LANES
+    chunks = width // step
     quarter = width // pieces
     hops = (n - 1) * pieces
     seqs = src_len.shape[1]
@@ -614,8 +614,11 @@
     def sec_copy(chunk, p):
         return remote(
             own.at[p, chunk], other.at[p, chunk],
-            sec_send.at[chunk, p], sec_recv.at[chunk, p], section=1 - sec,
-        )
+            sec_send, sec_recv.at[p], section=1 - sec,
+        )
+
+    def sec_all(p):
+        return remote(own.at[p], other.at[p], sec_send, sec_recv.at[p], section=1 - sec)
 
     def plane(view, send, recv, kind):
         small = part // 2
@@ -623,11 +626,11 @@
         size = (part, part, small, small)[kind]
         target = (near_x, near_y, near_y, near_x)[kind]
         ref = view(pl.ds(pl.multiple_of(start, small), size))
-        return remote(ref, ref, send.at[kind], recv.at[kind], mp=target)
+        return remote(ref, ref, send, recv.at[kind], mp=target)
 
     def px_copy(src, q, kind):
         return plane(
-            lambda at: xall.at[src, at, span(q)], px_send.at[src, q], px_recv.at[src, q], kind
+            lambda at: xall.at[src, at, span(q)], px_send.at[src], px_recv.at[src, q], kind
         )
 
     def za_copy(which, j):
@@ -651,12 +654,18 @@
         at = pl.ds(pl.multiple_of(d * step, step), step)
         return remote(
             partial.at[pl.ds(pl.multiple_of(peer * part, part), part), at],
-            landed.at[j, :, at], rs_send.at[j, d], rs_recv.at[j, d], mp=peer,
+            landed.at[j, :, at], rs_send, rs_recv.at[j], mp=peer,
+        )
+
+    def scatter_all(j):
+        peer = lax.rem(col + j, m)
+        return remote(
+            partial.at[pl.ds(0, part), :], landed.at[j], rs_send, rs_recv.at[j], mp=peer
         )
 
     def gather(kind):
         if kind > 1:
-            return plane(lambda at: result.at[at, :], ag_send, ag_recv, kind)
+            return plane(lambda at: result.at[at, :], ag_send.at[kind], ag_recv, kind)
         return remote(
             rest, result.at[band, :], ag_send.at[kind], ag_recv.at[kind],
             mp=(near_x, near_y)[kind],
@@ -831,8 +840,7 @@
             unit(axis, p, lax.rem(me + j, n))
 
     def ready(p):
-        for c in range(n):
-            sec_copy(c, p).wait_recv()
+        sec_all(p).wait_recv()
 
     def reduce_own(which_all):
         @pl.loop(0, chunks, unroll=2)
@@ -853,8 +861,7 @@
         xf = x[band, :].astype(f32)
         scale = lax.rsqrt(jnp.mean(xf * xf, axis=-1, keepdims=True) + EPS)
         for j in range(1, m):
-            for d in range(chunks):
-                scatter(j, d).wait_recv()
+            scatter_all(j).wait_recv()
         dnorm = total[band, :]
         for j in range(1, m):
             dnorm = dnorm + landed[j].astype(f32)
@@ -884,6 +891,45 @@
                         )
                     sec_copy(source(way, s), p).start()
 
+    def drain_source():
+        @pl.loop(0, hops)
+        def _(i):
+            s, q = i // pieces, i % pieces
+            for way in (0, 1):
+                pl.when(line_ok(way, s))(lambda way=way: zx_copy(way, s, q).wait_send())
+
+                @pl.when(jnp.logical_and(got(way, s), q == 0))
+                def _():
+                    src = source(way, s)
+                    ref = xall.at[src, pl.ds(0, 3 * part), :]
+                    remote(
+                        ref, ref, px_send.at[src], px_recv.at[src, 0, 0], mp=near_x
+                    ).wait_send()
+
+        for which in (0, 1):
+            keep_all(which).wait()
+
+    def drain_target():
+        for which in (0, 1):
+            keep_slice(which).wait()
+            for j in range(1, n):
+                za_copy(which, j).wait_send()
+                ref = (mine_a, mine_b)[which].at[0, pl.ds(0, 3 * part), :]
+                remote(
+                    ref, ref, sl_send.at[which, j], sl_recv.at[which, j, 0], mp=near_x
+                ).wait_send()
+                for kind in (2, 3):
+                    sl_copy(which, j, kind).wait_recv()
+        for p in range(pieces):
+            for s in range(n - 1):
+                for way in (0, 1):
+                    pl.when(line_ok(way, s))(
+                        lambda way=way, s=s, p=p: line_copy(way, s, p).wait_send()
+                    )
+
+    def drain_section():
+        remote(own, other, sec_send, sec_recv.at[0], section=1 - sec).wait_send()
+
     @pl.when(encoder)
     def _():
         lags = (0, 2, 5, 4 + pieces)
@@ -917,22 +963,13 @@
             for which in (0, 1):
                 grad_out(which, p).start()
             pl.when(p == 1)(finish_own)
-            pl.when(p == 2)(relay_own)
-
-
-        @pl.loop(0, hops)
-        def _(i):
-            s, q = i // pieces, i % pieces
-            for way in (0, 1):
-                pl.when(line_ok(way, s))(lambda way=way: zx_copy(way, s, q).wait_send())
-
-                @pl.when(got(way, s))
-                def _():
-                    for kind in range(4):
-                        px_copy(source(way, s), q, kind).wait_send()
-
-        for which in (0, 1):
-            keep_all(which).wait()
+
+            @pl.when(p == 2)
+            def _():
+                drain_source()
+                drain_section()
+                relay_own()
+
 
     @pl.when(decoder)
     def _():
@@ -969,29 +1006,18 @@
             for which in (0, 1):
                 grad_out(which, p).start()
             pl.when(p == 1)(finish_own)
-            pl.when(p == 2)(relay_own)
-
-        for which in (0, 1):
-            keep_slice(which).wait()
-            for j in range(1, n):
-                za_copy(which, j).wait_send()
-                for kind in range(4):
-                    sl_copy(which, j, kind).wait_send()
-                for kind in (2, 3):
-                    sl_copy(which, j, kind).wait_recv()
-        for p in range(pieces):
-            for s in range(n - 1):
-                for way in (0, 1):
-                    pl.when(line_ok(way, s))(
-                        lambda way=way, s=s, p=p: line_copy(way, s, p).wait_send()
-                    )
-
-    for p in range(pieces):
-        for c in range(n):
-            sec_copy(c, p).wait_send()
-    for j in range(1, m):
-        for d in range(chunks):
-            scatter(j, d).wait_send()
+
+            @pl.when(p == 2)
+            def _():
+                drain_target()
+                drain_section()
+                relay_own()
+
+    sent = pl.ds(0, (m - 1) * part)
+    remote(
+        partial.at[sent, :], partial.at[sent, :], rs_send, rs_recv.at[0],
+        mp=lax.rem(col + 1, m),
+    ).wait_send()
     for kind in range(4):
         gather(kind).wait_send()
     for kind in (2, 3):
@@ -1023,8 +1049,9 @@
     ]
     pair = lambda *shape: [dma(shape), dma(shape)]
     sems = [pltpu.SemaphoreType.REGULAR, dma((6,)), dma((2, pieces)), dma((3,)), dma((2, pieces))]
-    sems += pair(2, n, pieces) + pair(n, pieces, 4) + pair(2, n, pieces) + pair(n, pieces)
-    sems += pair(2, n) + pair(2, n, 4) + pair(m, chunks) + pair(4)
+    sems += pair(2, n - 1, pieces) + [dma((n,)), dma((n, pieces, 4))]
+    sems += pair(2, n - 1, pieces) + [dma(()), dma((pieces,))]
+    sems += pair(2, n) + [dma((2, n)), dma((2, n, 4))] + [dma(()), dma((m,))] + pair(4)
     return buffers, sems
 
 

time: 80.2 us -> 78.3 us (0.976)
  Pallas kernels: 79.4 us -> 77.5 us
    pallas_call x1, Pallas kernels: 73.6 us -> 71.8 us  [fused(): pl.pallas_call(functools.partial(fused_kernel, n, m), out_shape=(jax.Shap...]
where the time goes in v4:
time: 78.3 us; the launch traced here: 78.2 us
  Pallas kernels  77.5 us (99%)
    pallas_call x1, Pallas kernels, fused(): pl.pallas_call(functools.partial(fused_kernel, n, m), out_shape=(jax.Shap...  71.8 us
    pallas_call x1, Pallas kernels, grads(): pl.pallas_call(grads_kernel, out_shape=(jax.ShapeDtypeStruct((1, cols, in...  5.75 us

profile of v4, /device:TPU:0, one launch (start us, length us, event | category | flops | bytes accessed | tf_op | source)
XLA Modules:
  0.0 78.2 jit_solution(3017117059077041228)
XLA Ops:
  0.6 71.8 %fused.1 = (bf16[128,4096]{1,0:T(8,128)(2,1)}, bf16[4,128,1024]{2,1,0:T(8,128)(2,1)}, bf16[4,128,1024]{2,1,0:T(8,128)(2,1)}, bf16[4,128,1024]{2,1,0:T(8,128)(2,1)}, bf16[4,128,1024]{2,1,0:T(8,128)(2,1)}) custom-call(bf16[1,128,4096]{2,1,0:T(8,128)(2,1)} %x_hbm.1, bf16[128,4096]{1,0:T(8,128)(2,1)} %cot_hbm.1, f32[1,4096]{1,0:T(1,128)} %gain_hbm.1, ...), custom_call_target="tpu_custom_call" | custom-call | tf_op jit(solution)/shard_map/fused/pallas_call | solution.py:1079
  72.4 5.7 %grads.1 = (f32[1,1024,1024]{2,1,0:T(8,128)}, f32[1,1024,1024]{2,1,0:T(8,128)}, bf16[1,128,4096]{2,1,0:T(8,128)(2,1)}) custom-call(bf16[512,1024]{1,0:T(8,128)(2,1)} %bitcast.6, bf16[512,1024]{1,0:T(8,128)(2,1)} %bitcast.7, bf16[512,1024]{1,0:T(8,128)(2,1)} %bitcast.4, bf16[512,1024]{1,0:T(8,128)(2,1)} %bitcast.5, bf16[128,4096]{1,0:T(8,128)(2,1)} %get-tuple-element.15.states_in), custom_call_target="tpu_custom_call" | custom-call | tf_op jit(solution)/shard_map/grads/pallas_call | solution.py:1141
